TPU v7x, 512 devices: a whole 4x4x16 slice. The times are simulated.
512 devices in a mesh: vocab: 64 (over y, z), tp: 8 (over x, core).
Axes of the slice: x: 4, y: 4, z: 16, core: 2. Of those that a mesh axis runs over, the one named last changes fastest.
Arguments:
- residual: bfloat16 [512, 8192], P(None, 'tp'), may hold values from -64 to 64
- activation: bfloat16 [512, 16384], P('tp', 'vocab'), may hold values from -6 to 6
- down_weight: bfloat16 [16384, 8192], P('vocab', 'tp'), may hold values from -0.046875 to 0.046875
- norm_gain: float32 [8192], P('tp'), may hold values from 0.5 to 1.5
- head_weight: bfloat16 [8192, 81920], P('tp', 'vocab'), may hold values from -1 to 1
- allowed: int32 [512, 32], replicated, may hold values from 0 to 639, as said below
- tokens: int32 [512], P('tp'), may hold values from 0 to 81919, as said below
- lengths: int32 [4], replicated, may hold values from 1 to 128, as said below
- advantage_code: int32 [4], replicated, may hold values from -64 to 64
Outputs:
- policy_loss: float32 [], replicated
- down_gradient: bfloat16 [16384, 8192], P('vocab', 'tp')
- activation_gradient: bfloat16 [512, 16384], P('tp', 'vocab')
Inputs may be any that keep to these rules, and one draw needn't show every extreme that they name: `allowed`: block numbers may repeat within a row; among the blocks v * 10 to (v + 1) * 10 - 1 of any one vocab index v, a row lists at most 4 different ones, and some row lists exactly 4. `tokens`: each row's token lies in a block that its row lists. `lengths`: at least one response has length 128.
All inputs are finite; a program needn't handle non-finite values.
Results may differ from a plain program's by a relative error of at most 0.0059.
Values may be sent and summed in bfloat16 or wider, within the bound.
A program may use at most 64 MiB of HBM per device.

v0:
```python
import jax
import jax.numpy as jnp
from jax import lax
from jax.sharding import PartitionSpec as P

D = 8192
BLK = 128
SEQ = 128


def lookup_small(table, index_row):
    match = index_row[:, None] == jnp.arange(table.shape[0], dtype=jnp.int32)[None, :]
    return jnp.sum(jnp.where(match, table[None, :], 0), axis=1)


def body(
    residual,
    activation,
    down_weight,
    norm_gain,
    head_weight,
    allowed,
    tokens,
    lengths,
    advantage_code,
):
    all_rows = residual.shape[0]
    tp_count = lax.axis_size("tp")
    row_share = all_rows // tp_count
    vocab_index = lax.axis_index("vocab")
    tp_index = lax.axis_index("tp")
    cols_dev = head_weight.shape[1]
    blocks_dev = cols_dev // BLK
    activation_rows = lax.all_gather(activation, "tp", axis=0, tiled=True)
    rows_in = activation_rows
    mixed_term = lax.psum(
        jnp.dot(rows_in, down_weight, preferred_element_type=jnp.float32), "vocab"
    )
    hidden = residual.astype(jnp.float32) + mixed_term
    square_total = lax.psum(jnp.sum(hidden * hidden, axis=1), "tp")
    inv_rms = lax.rsqrt(square_total[:, None] / D + 1e-06)
    normed = (hidden * inv_rms * norm_gain).astype(jnp.bfloat16)
    first_local = tp_index * row_share
    row_ids = first_local + jnp.arange(row_share, dtype=jnp.int32)
    local_blocks = jnp.arange(blocks_dev, dtype=jnp.int32)
    block_ids = vocab_index * blocks_dev + local_blocks
    block_all = jnp.any(allowed[:, :, None] == block_ids[None, None, :], axis=1)
    rows_in = normed
    logits = lax.psum_scatter(
        jnp.dot(rows_in, head_weight, preferred_element_type=jnp.float32),
        "tp",
        scatter_dimension=0,
        tiled=True,
    )
    local_ok = lax.dynamic_slice_in_dim(block_all, first_local, row_share, 0)
    permitted = jnp.repeat(local_ok, BLK, axis=1)
    column_ids = (vocab_index * cols_dev + jnp.arange(cols_dev, dtype=jnp.int32))[None, :]
    local_peak = jnp.max(jnp.where(permitted, logits, -1e30), axis=1)
    onehot = column_ids == tokens[:, None]
    local_target = jnp.sum(jnp.where(onehot, logits, 0.0), axis=1)
    row_peak = lax.pmax(local_peak, "vocab")
    local_total = jnp.sum(jnp.where(permitted, jnp.exp(logits - row_peak[:, None]), 0.0), axis=1)
    exp_total, target = lax.psum((local_total, local_target), "vocab")
    log_prob = target - row_peak - jnp.log(exp_total)
    response = row_ids // SEQ
    valid_row = row_ids % SEQ < lookup_small(lengths, response)
    advantage = lookup_small(advantage_code, response).astype(jnp.float32) / 32.0
    weight = jnp.where(valid_row, advantage, 0.0)
    objective = lax.psum(jnp.sum(weight * log_prob), "tp")
    policy_loss = -objective / jnp.sum(lengths).astype(jnp.float32)
    probability = (
        jnp.where(permitted, jnp.exp(logits - row_peak[:, None]), 0.0) / exp_total[:, None]
    )
    dlogits = (weight[:, None] * (probability - onehot.astype(jnp.float32))).astype(jnp.bfloat16)
    dense_piece = lax.all_gather(dlogits, "tp", axis=0, tiled=True)
    dnormed_term = lax.dot_general(
        dense_piece, head_weight, (((1,), (1,)), ((), ())), preferred_element_type=jnp.float32
    )
    dnormed = lax.psum(dnormed_term, "vocab")
    gained = dnormed * norm_gain
    gain_dot = lax.psum(jnp.sum(gained * hidden, axis=1), "tp")
    dhidden = (
        inv_rms * gained - hidden * (inv_rms * inv_rms * inv_rms) * gain_dot[:, None] / D
    ).astype(jnp.bfloat16)
    down_gradient = lax.dot_general(
        activation_rows, dhidden, (((0,), (0,)), ((), ())), preferred_element_type=jnp.float32
    ).astype(jnp.bfloat16)
    rows_in = dhidden
    activation_gradient = lax.psum_scatter(
        lax.dot_general(
            rows_in, down_weight, (((1,), (1,)), ((), ())), preferred_element_type=jnp.float32
        ),
        "tp",
        scatter_dimension=0,
        tiled=True,
    ).astype(jnp.bfloat16)
    return (policy_loss, down_gradient, activation_gradient)


def solution(mesh):
    in_specs = (
        P(None, "tp"),
        P("tp", "vocab"),
        P("vocab", "tp"),
        P("tp"),
        P("tp", "vocab"),
        P(),
        P("tp"),
        P(),
        P(),
    )
    out_specs = (P(), P("vocab", "tp"), P("tp", "vocab"))
    return jax.shard_map(body, mesh=mesh, in_specs=in_specs, out_specs=out_specs, check_vma=False)
```

profile of v0, /device:TPU:1, one launch (start us, length us, event | category | flops | bytes accessed | tf_op | source)
XLA Modules:
  0.0 1017.0 jit_solution(12101272680856169493)
XLA Ops:
  7.2 19.9 %all_gather.6 = bf16[512,256]{1,0:T(8,128)(2,1)S(1)} all-gather(bf16[64,256]{1,0:T(8,128)(2,1)} %param.10), channel_id=1, replica_groups=mesh['vocab'=64,'tp'=8] {'tp'}, dimensions={0}, use_global_device_ids=true | all-gather | bytes 294912 | tf_op jit(solution)/shard_map/all_gather | solution.py:34
  27.1 2.8 fusion.9
  29.9 269.5 %all-reduce.5.cloned.1.call-done = f32[512,1024]{1,0:T(8,128)} async-done(((f32[512,1024]{1,0:T(8,128)}), f32[512,1024]{1,0:T(8,128)}) %all-reduce.5.cloned.1.call-update) | async-done | bytes 2097168 | tf_op jit(solution)/shard_map/psum | solution.py:36
  299.5 2.2 multiply_reduce_fusion.1
  301.7 22.1 %psum.50 = f32[512]{0:T(512)S(1)} all-reduce(f32[512]{0:T(512)S(1)} %multiply_reduce_fusion.1), channel_id=1, replica_groups=mesh['vocab'=64,'tp'=8] {'tp'}, use_global_device_ids=true, to_apply=%region_4.0 | all-reduce | flops 512 | bytes 4096 | tf_op jit(solution)/shard_map/psum | solution.py:40
  323.8 4.9 fusion.1
  328.9 0.7 copy-done.3
  329.6 0.2 compare_reduce_fusion
  329.7 0.1 constant_dynamic-slice_fusion
  329.8 0.1 copy.16
  330.0 0.1 select_reduce_fusion.1
  330.1 32.3 %reduce-scatter.3.cloned.1.call-done = f32[64,1280]{1,0:T(8,128)} async-done(((f32[512,1280]{1,0:T(8,128)}), f32[64,1280]{1,0:T(8,128)}) %reduce-scatter.3.cloned.1.call-update) | async-done | bytes 327696 | tf_op jit(solution)/shard_map/reduce_scatter | solution.py:49
  362.4 0.2 broadcast_in_dim.57
  362.6 1.1 select_reduce_fusion
  363.7 115.8 %pmax.7 = f32[64]{0:T(128)S(1)} all-reduce(f32[64]{0:T(128)S(1)} %select_reduce_fusion), channel_id=1, replica_groups=mesh['vocab'=64,'tp'=8] {'vocab'}, use_global_device_ids=true, to_apply=%region_10.11 | all-reduce | flops 64 | bytes 512 | tf_op jit(solution)/shard_map/pmax | solution.py:61
  479.6 1.2 fusion.4
  480.8 110.5 %all-reduce = (f32[64]{0:T(128)S(1)}, f32[64]{0:T(128)S(1)}) all-reduce(f32[64]{0:T(128)S(1)} %get-tuple-element.13, f32[64]{0:T(128)S(1)} %get-tuple-element.12), channel_id=1, replica_groups=mesh['vocab'=64,'tp'=8] {'vocab'}, use_global_device_ids=true, to_apply=%region_12.13 | all-reduce | flops 128 | bytes 1024 | tf_op jit(solution)/shard_map/psum | solution.py:63
  591.3 0.6 multiply_reduce_fusion.2
  592.0 1.8 fusion.7
  593.9 77.1 %all-gather.2.cloned.1.call-done = bf16[512,1280]{1,0:T(8,128)(2,1)} async-done(((bf16[64,1280]{1,0:T(8,128)(2,1)}), bf16[512,1280]{1,0:T(8,128)(2,1)}) %all-gather.2.cloned.1.call-update) | async-done | bytes 1310736 | tf_op jit(solution)/shard_map/all_gather | solution.py:75
  671.0 4.2 fusion.10
  675.3 271.2 %all-reduce.7.cloned.1.call-done = f32[512,1024]{1,0:T(8,128)} async-done(((f32[512,1024]{1,0:T(8,128)}), f32[512,1024]{1,0:T(8,128)}) %all-reduce.7.cloned.1.call-update) | async-done | bytes 2097168 | tf_op jit(solution)/shard_map/psum | solution.py:79
  946.4 2.9 multiply_reduce_fusion
  949.3 22.8 %all-reduce.1 = (f32[]{:T(128)}, f32[512]{0:T(512)S(1)}) all-reduce(f32[]{:T(128)} %get-tuple-element.20, f32[512]{0:T(512)S(1)} %multiply_reduce_fusion), channel_id=1, replica_groups=mesh['vocab'=64,'tp'=8] {'tp'}, use_global_device_ids=true, to_apply=%region_14.15 | all-reduce | flops 513 | bytes 4104 | tf_op jit(solution)/shard_map/psum | solution.py:69
  972.1 3.2 subtract_convert_fusion
  975.3 1.0 copy-done.1
  976.3 1.3 fusion.11
  977.6 0.6 reduce_sum.78
  979.6 1.7 fusion
  981.3 1.0 copy.17
  982.3 25.6 %reduce-scatter.5.cloned.1.call-done = f32[64,256]{1,0:T(8,128)} async-done(((f32[512,256]{1,0:T(8,128)}), f32[64,256]{1,0:T(8,128)}) %reduce-scatter.5.cloned.1.call-update) | async-done | bytes 65552 | tf_op jit(solution)/shard_map/reduce_scatter | solution.py:89
  1007.9 1.5 convert_element_type.43
  (28 shorter events, 0.4 us)
Async XLA Ops:
  7.2 316.6 %copy-start = (bf16[1024,1280]{1,0:T(8,128)(2,1)S(1)}, bf16[1024,1280]{1,0:T(8,128)(2,1)}, u32[]{:S(2)}) copy-start(bf16[1024,1280]{1,0:T(8,128)(2,1)} %param.13) | copy-start | bytes 7864324
  7.2 292.3 %all-reduce.5.cloned.1.call-start = ((), (), s32[]{:S(2)}) async-start(), calls=%async_computation.2 | async-start | bytes 4194304 | tf_op jit(solution)/shard_map/psum | solution.py:36
  29.9 293.9 %copy-start.4 = (f32[1024]{0:T(1024)S(1)}, f32[1024]{0:T(1024)}, u32[]{:S(2)}) copy-start(f32[1024]{0:T(1024)} %param.12) | copy-start | bytes 12292
  29.9 332.5 %reduce-scatter.3.cloned.1.call-start = ((), (), s32[]{:S(2)}) async-start(), calls=%async_computation.3 | async-start | bytes 2949120 | tf_op jit(solution)/shard_map/reduce_scatter | solution.py:49
  328.8 0.8 copy-start.3
  328.8 1.2 copy-start.6
  328.8 1.2 copy-start.7
  328.8 150.8 %copy-start.5 = (s32[64]{0:T(128)S(1)}, s32[64]{0:T(128)}, u32[]{:S(2)}) copy-start(s32[64]{0:T(128)} %param.15) | copy-start | bytes 772
  328.8 342.2 %all-gather.2.cloned.1.call-start = ((), (), s32[]{:S(2)}) async-start(), calls=%async_computation.4 | async-start | bytes 1474560 | tf_op jit(solution)/shard_map/all_gather | solution.py:75
  593.8 352.6 %all-reduce.7.cloned.1.call-start = ((), (), s32[]{:S(2)}) async-start(), calls=%async_computation.5 | async-start | bytes 4194304 | tf_op jit(solution)/shard_map/psum | solution.py:79
  675.2 332.7 %reduce-scatter.5.cloned.1.call-start = ((), (), s32[]{:S(2)}) async-start(), calls=%async_computation.6 | async-start | bytes 589824 | tf_op jit(solution)/shard_map/reduce_scatter | solution.py:89
  972.1 4.2 copy-start.2
  975.3 1.0 copy-start.1
Sparse Core Ops, SparseCore 0:
  30.0 269.4 all-reduce.4
  328.9 33.4 reduce-scatter.2
  593.9 76.9 all-gather.1
  675.3 271.0 all-reduce.6
  977.8 30.0 reduce-scatter.4
where the time goes:
time: 1020 us
  waiting for transfers between devices  676 us (66%)
  blocking collectives  291 us (29%)
  between operations  16.4 us (2%)
  other arithmetic  15.4 us (2%)
  matrix products  14.9 us (1%)
    psum x1, waiting for transfers between devices, body(): dnormed = lax.psum(dnormed_term, 'vocab')  271 us
    psum x1, waiting for transfers between devices, body(): lax.psum(jnp.dot(rows_in, down_weight, preferred_element_type=jnp.float32...  270 us
    pmax x1, blocking collectives, body(): row_peak = lax.pmax(local_peak, 'vocab')  116 us
    psum x1, blocking collectives, body(): exp_total, target = lax.psum((local_total, local_target), 'vocab')  111 us
    all_gather x1, waiting for transfers between devices, body(): dense_piece = lax.all_gather(dlogits, 'tp', axis=0, tiled=True)  77.1 us
    reduce_scatter x1, waiting for transfers between devices, body(): lax.psum_scatter(jnp.dot(rows_in, head_weight, preferred_element_type=jnp...  32.3 us
    reduce_scatter x1, waiting for transfers between devices, body(): lax.psum_scatter(lax.dot_general(rows_in, down_weight, (((1,), (1,)), (()...  25.6 us
    psum x1, blocking collectives, body(): objective = lax.psum(jnp.sum(weight * log_prob), 'tp')  22.8 us
  transfers between devices with their start and end apart: 5, of which 5 were waited for; matrix products, arithmetic and copies ran while one was open for 0% of the time, Pallas kernels for 0%

commit v1 on v0

v1 whole, which is shorter than its diff:
```python
import jax
import jax.numpy as jnp
from jax import lax
from jax.experimental import pallas as pl
from jax.experimental.pallas import tpu as pltpu
from jax.sharding import PartitionSpec as P

MESH = pl.DeviceIdType.MESH
F32 = jnp.float32
BF16 = jnp.bfloat16
D = 8192
BLK = 128
CAP = 4
NB = 10
NY = 4
NZ = 16
NX = 4
NEG = -1e30
NC = 2
CW = 1024 // NC
DW = CAP * BLK + BLK
N_SEND = 200
NT = (((1,), (1,)), ((), ()))


def kernel(
    res_hbm,
    act_hbm,
    w_hbm,
    gain_ref,
    head_hbm,
    allowed_ref,
    tok_ref,
    len_ref,
    adv_ref,
    loss_ref,
    dg_ref,
    ag_ref,
    res,
    act,
    actt,
    w,
    head,
    slotb,
    own,
    s1,
    ry1,
    t1,
    s1a,
    ra1,
    t1a,
    s1b,
    rb1,
    hid,
    ssq,
    nrm,
    s2,
    ry2,
    s2a,
    ra2,
    s2b,
    rb2,
    dhg,
    lhs,
    lb,
    lp,
    lpr,
    lx,
    lxr,
    lg,
    stz,
    sty,
    dl,
    gs,
    lhs2,
    dh,
    ags,
    agr,
    los,
    lsem,
    ssem,
    rsem,
):
    v = lax.axis_index("vocab")
    t = lax.axis_index("tp")
    y = v // NZ
    z = v % NZ
    x = t // 2
    c = t % 2
    k0 = z % 4
    m0 = z // 4

    def dev_y(d):
        return (((y + d) % NY) * NZ + z, t)

    def dev_z(d):
        return (y * NZ + (z + d) % NZ, t)

    def dev_t(d):
        return (v, (t + d) % 8)

    def dev_x(d):
        return (v, ((x + d) % NX) * 2 + c)

    partner = (v, x * 2 + (1 - c))

    barrier = pltpu.get_barrier_semaphore()
    peers = (
        [dev_t(d) for d in range(1, 8)]
        + [dev_y(d) for d in range(1, 4)]
        + [dev_z(d) for d in (1, 2, 4, 8, 12, 14, 15)]
    )
    for dev in peers:
        pl.semaphore_signal(barrier, inc=1, device_id=dev, device_id_type=MESH)

    loads = [
        pltpu.make_async_copy(act_hbm, act.at[t], lsem.at[0]),
        pltpu.make_async_copy(w_hbm, w, lsem.at[1]),
        pltpu.make_async_copy(res_hbm.at[y * 16 + k0 * 4 + m0], res, lsem.at[2]),
        pltpu.make_async_copy(head_hbm, head, lsem.at[3]),
    ]
    for copy in loads:
        copy.start()

    first_block = v * NB

    def prep(i, carry):
        rows = pl.ds(pl.multiple_of(i * 128, 128), 128)
        listed = allowed_ref[rows, :]
        run = jnp.zeros((128, 1), F32)
        for b in range(NB):
            hit = jnp.max(
                jnp.where(listed == first_block + b, 1.0, 0.0).astype(F32), axis=1, keepdims=True
            )
            slot = jnp.where(hit > 0.5, run, 99.0)
            run = run + hit
            slotb[b, rows, :] = jnp.broadcast_to(slot, (128, 128))
        return carry

    lax.fori_loop(0, 4, prep, 0)

    sends = []
    count = [0]

    def rcopy(src, dst, dev):
        i = count[0]
        count[0] += 1
        copy = pltpu.make_async_remote_copy(
            src_ref=src,
            dst_ref=dst,
            send_sem=ssem.at[i],
            recv_sem=rsem.at[i],
            device_id=dev,
            device_id_type=MESH,
        )
        copy.start()
        sends.append(copy)
        return copy

    loads[0].wait()
    pl.semaphore_wait(barrier, len(peers))

    a_in = {}
    for d in (4, 3, 5, 2, 6, 1, 7):
        a_in[d] = rcopy(act.at[t], act.at[t], dev_t(d))
    loads[1].wait()
    for d in range(1, 8):
        a_in[d].wait_recv()

    def act_rows(yb):
        return jnp.concatenate([act[2 * yb], act[2 * yb + 1]], axis=0)

    def rs_y(s, ry, d, yb):
        return [
            rcopy(
                s.at[pl.ds(n * 64 + yb * 16, 16)],
                ry.at[pl.ds(((d - 1) * NC + n) * 16, 16)],
                dev_y(d),
            )
            for n in range(NC)
        ]

    def rs_rest(y_in, ry, sa, ra, sb, rb, use):
        a_in, b_in = [], []
        for n in range(NC):
            total = own[n * 16 : (n + 1) * 16]
            for d in (1, 3, 2):
                y_in[d][n].wait_recv()
            for d in (1, 3, 2):
                q = (d - 1) * NC + n
                total = total + ry[q * 16 : (q + 1) * 16].astype(F32)
            t1[n * 16 : (n + 1) * 16] = total
            sa[n * 16 : (n + 1) * 16] = total.astype(BF16)
            far = 2 if n % 2 == 0 else 14
            a_in.append(
                [
                    rcopy(
                        sa.at[pl.ds(n * 16 + ((k0 + dz) % 4) * 4, 4)],
                        ra.at[pl.ds((j * NC + n) * 4, 4)],
                        dev_z(dz),
                    )
                    for j, dz in ((2, far), (0, 1), (1, 15))
                ]
            )
        for n in range(NC):
            for copy in a_in[n]:
                copy.wait_recv()
            total = t1[pl.ds(n * 16 + k0 * 4, 4)]
            for j in range(3):
                q = j * NC + n
                total = total + ra[q * 4 : (q + 1) * 4].astype(F32)
            t1a[n * 4 : (n + 1) * 4] = total
            sb[n * 4 : (n + 1) * 4] = total.astype(BF16)
            b_in.append(
                [
                    rcopy(
                        sb.at[pl.ds(n * 4 + (m0 + dm) % 4, 1)],
                        rb.at[pl.ds((dm - 1) * NC + n, 1)],
                        dev_z(4 * dm),
                    )
                    for dm in (2, 1, 3)
                ]
            )
        for n in range(NC):
            for copy in b_in[n]:
                copy.wait_recv()
            total = t1a[n * 4 + m0]
            for dm in range(3):
                total = total + rb[dm * NC + n].astype(F32)
            use(n, total)

    def gather(g):
        base = y * 16
        b_in, y_in = [], []

        def to_y(n, cls):
            rows = pl.ds(n * 64 + base + cls * 4, 4)
            return {d: rcopy(g.at[rows], g.at[rows], dev_y(d)) for d in (2, 1, 3)}

        for n in range(NC):
            row = pl.ds(n * 64 + base + k0 * 4 + m0, 1)
            b_in.append([rcopy(g.at[row], g.at[row], dev_z(4 * dm)) for dm in (2, 1, 3)])
        a_in = []
        for n in range(NC):
            for copy in b_in[n]:
                copy.wait_recv()
            rows = pl.ds(n * 64 + base + k0 * 4, 4)
            far = 2 if n % 2 == 0 else 14
            a_in.append([rcopy(g.at[rows], g.at[rows], dev_z(dz)) for dz in (far, 1, 15)])
            y_in.append([to_y(n, k0)])
        for n in range(NC):
            for j, dk in ((1, 3), (2, 1), (0, 2)):
                a_in[n][j].wait_recv()
                y_in[n].append(to_y(n, (k0 + dk) % 4))
        return y_in

    def gathered(g, y_in, d):
        if d > 0:
            for n in range(NC):
                for part in y_in[n]:
                    part[d].wait_recv()
        yb = (y + 4 - d) % 4
        pieces = [
            g[pl.ds(n * 64 + yb * 16, 16)].astype(F32).reshape(128, CW).astype(BF16)
            for n in range(NC)
        ]
        return yb, jnp.concatenate(pieces, axis=1)

    y_in = {}
    for d in (2, 1, 3, 0):
        yb = (y + d) % 4
        for n in range(NC):
            part = jnp.dot(act_rows(yb), w[:, n * CW : (n + 1) * CW], preferred_element_type=F32)
            part = part.reshape(16, 8, CW)
            if d == 0:
                own[n * 16 : (n + 1) * 16] = part
            else:
                s1[pl.ds(n * 64 + yb * 16, 16)] = part.astype(BF16)
        if d > 0:
            y_in[d] = rs_y(s1, ry1, d, yb)

    for i in range(8):
        actt[:, i * 64 : (i + 1) * 64] = act[i].astype(F32).T.astype(BF16)
    loads[2].wait()

    def use_hidden(n, total):
        hid[:, n * CW : (n + 1) * CW] = res[:, n * CW : (n + 1) * CW].astype(F32) + total

    rs_rest(y_in, ry1, s1a, ra1, s1b, rb1, use_hidden)

    h = hid[...]
    ssq[t] = jnp.broadcast_to(jnp.sum(h * h, axis=1, keepdims=True), (8, 128))
    ss_in = [rcopy(ssq.at[t], ssq.at[t], dev_t(d)) for d in (4, 3, 5, 2, 6, 1, 7)]
    for copy in ss_in:
        copy.wait_recv()
    square = ssq[0]
    for i in range(1, 8):
        square = square + ssq[i]
    inv_rms = lax.rsqrt(square[:, :1] / D + 1e-06)
    mine = y * 16 + k0 * 4 + m0
    for n in range(NC):
        cols = slice(n * CW, (n + 1) * CW)
        nrm[n * 64 + mine] = (hid[:, cols] * inv_rms * gain_ref[:, cols]).astype(BF16)
    y_in = gather(nrm)
    loads[3].wait()

    x_in = {}
    order = (0, 1, 3, 2)
    p_in = []
    for d in order:
        yb, block = gathered(nrm, y_in, d)
        lhs[...] = block

        def columns(j, carry):
            cols = pl.ds(pl.multiple_of(j * 256, 256), 256)
            lb[:, cols] = jnp.dot(lhs[...], head[:, cols], preferred_element_type=F32)
            return carry

        lax.fori_loop(0, 5, columns, 0)

        def compact(half, dst):
            rows = pl.ds(pl.multiple_of(half * 64, 64), 64)
            mask_rows = pl.ds(pl.multiple_of(yb * 128 + half * 64, 64), 64)
            out = [jnp.zeros((64, 128), F32) for _ in range(CAP)]
            for b in range(NB):
                slot = slotb[b, mask_rows, :]
                val = lb[rows, b * BLK : (b + 1) * BLK]
                for s in range(CAP):
                    out[s] = jnp.where(slot == float(s), val, out[s])
            for s in range(CAP):
                dst[:, s * BLK : (s + 1) * BLK] = out[s]

        compact(1 - c, lp.at[yb])
        p_in.append(rcopy(lp.at[yb], lpr.at[yb], partner))
        compact(c, lx.at[yb])
        if d != order[0]:
            combine(p_prev, yb_prev)
        p_prev, yb_prev = p_in[-1], yb

        def combine(copy, row_block):
            copy.wait_recv()
            lx[row_block] = lx[row_block] + lpr[row_block]

    combine(p_prev, yb_prev)
    x_in = {d: rcopy(lx.at[(x + d) % 4], lxr.at[d - 1], dev_x(d)) for d in (2, 1, 3)}
    total = lx[x]
    for d in (1, 3, 2):
        x_in[d].wait_recv()
        total = total + lxr[d - 1]
    lg[...] = total

    own_rows = pl.ds(pl.multiple_of(t * 64, 64), 64)
    lane = lax.broadcasted_iota(jnp.int32, (64, 128), 1)
    eye = lane == lax.broadcasted_iota(jnp.int32, (64, 128), 0)

    def to_row(col):
        return jnp.sum(jnp.where(eye, col, 0.0), axis=0, keepdims=True)

    def to_col(row):
        return jnp.sum(jnp.where(eye, row, 0.0), axis=1, keepdims=True)

    tok = to_col(tok_ref[...].astype(F32)).astype(jnp.int32)
    tok_block = (tok >> 7) - first_block
    tok_lane = tok & 127
    seen = jnp.zeros((64, 128), F32)
    tok_slot = jnp.full((64, 128), 99.0, F32)
    for b in range(NB):
        slot = slotb[b, own_rows, :]
        seen = seen + jnp.where(slot < 50.0, 1.0, 0.0)
        tok_slot = jnp.where(tok_block == b, slot, tok_slot)

    peak = jnp.full((64, 128), NEG, F32)
    for s in range(CAP):
        peak = jnp.maximum(peak, jnp.where(seen > float(s), lg[:, s * BLK : (s + 1) * BLK], NEG))
    peak = jnp.max(peak, axis=1, keepdims=True)
    zero = jnp.zeros((64, 128), F32)
    tot, mom, tgt = zero, zero, zero
    for s in range(CAP):
        val = lg[:, s * BLK : (s + 1) * BLK]
        ok = seen > float(s)
        shifted = jnp.where(ok, val - peak, 0.0)
        e = jnp.where(ok, jnp.exp(shifted), 0.0)
        tot = tot + e
        mom = mom + e * shifted
        tgt = tgt + jnp.where((tok_slot == float(s)) & (lane == tok_lane), val, 0.0)
    tot = jnp.sum(tot, axis=1, keepdims=True)
    mom = jnp.sum(mom, axis=1, keepdims=True)
    tgt = jnp.sum(tgt, axis=1, keepdims=True)
    at = k0 * 4 + m0
    stz[at] = jnp.concatenate(
        [to_row(peak), to_row(tot), to_row(mom), to_row(tgt), jnp.zeros((4, 128), F32)], axis=0
    )
    b_in = [rcopy(stz.at[at], stz.at[at], dev_z(4 * dm)) for dm in (2, 1, 3)]
    for copy in b_in:
        copy.wait_recv()
    rows = pl.ds(k0 * 4, 4)
    a_in = [rcopy(stz.at[rows], stz.at[rows], dev_z(dz)) for dz in (2, 1, 15)]
    for copy in a_in:
        copy.wait_recv()

    def join(parts):
        top = parts[0][0:1]
        for p in parts[1:]:
            top = jnp.maximum(top, p[0:1])
        tot = jnp.zeros((1, 128), F32)
        mom = jnp.zeros((1, 128), F32)
        tgt = jnp.zeros((1, 128), F32)
        for p in parts:
            gap = p[0:1] - top
            scale = jnp.exp(gap)
            tot = tot + p[1:2] * scale
            mom = mom + scale * (p[2:3] + p[1:2] * gap)
            tgt = tgt + p[3:4]
        return top, tot, mom, tgt

    top, tot, mom, tgt = join([stz[i] for i in range(NZ)])
    sty[y] = jnp.concatenate([top, tot, mom, tgt, jnp.zeros((4, 128), F32)], axis=0)
    y_st = [rcopy(sty.at[y], sty.at[y], dev_y(d)) for d in (2, 1, 3)]
    for copy in y_st:
        copy.wait_recv()
    top, tot, mom, tgt = join([sty[i] for i in range(NY)])
    top, tot, mom, tgt = to_col(top), to_col(tot), to_col(mom), to_col(tgt)

    response = t // 2
    length = jnp.int32(0)
    code = jnp.int32(0)
    length_sum = jnp.int32(0)
    for i in range(4):
        length = jnp.where(response == i, len_ref[i], length)
        code = jnp.where(response == i, adv_ref[i], code)
        length_sum = length_sum + len_ref[i]
    position = c * 64 + lax.broadcasted_iota(jnp.int32, (64, 1), 0)
    weight = jnp.where(position < length, code.astype(F32) / 32.0, 0.0)
    log_prob = tgt - top - jnp.log(tot)
    part = jnp.sum(weight * log_prob, axis=0, keepdims=True)
    gdot = weight * (mom / tot - (tgt - top))
    for s in range(CAP):
        val = lg[:, s * BLK : (s + 1) * BLK]
        prob = jnp.where(seen > float(s), jnp.exp(val - top), 0.0) / tot
        hot = jnp.where((tok_slot == float(s)) & (lane == tok_lane), 1.0, 0.0)
        dl[t, :, s * BLK : (s + 1) * BLK] = (weight * (prob - hot)).astype(BF16)
    g_hi = gdot.astype(BF16).astype(F32)
    g_mid = (gdot - g_hi).astype(BF16).astype(F32)
    g_lo = gdot - g_hi - g_mid
    tail = jnp.where(lane == 0, g_hi, jnp.where(lane == 1, g_mid, jnp.where(lane == 2, g_lo, 0.0)))
    dl[t, :, CAP * BLK :] = tail.astype(BF16)

    dx_in = {d: rcopy(dl.at[t], dl.at[t], dev_x(d)) for d in (2, 1, 3)}
    d_in = {0: rcopy(dl.at[t], dl.at[t], partner)}
    for d in (1, 3, 2):
        dx_in[d].wait_recv()
        slot = ((x + 4 - d) % 4) * 2 + c
        d_in[d] = rcopy(dl.at[slot], dl.at[slot], partner)
    los[t] = jnp.broadcast_to(part, (8, 128))
    loss_in = [rcopy(los.at[t], los.at[t], dev_t(d)) for d in range(1, 8)]
    for d in range(4):
        d_in[d].wait_recv()

    y_in = {}
    for d in (2, 1, 3, 0):
        yb = (y + d) % 4
        for half in range(2):
            rows = slice(half * 64, (half + 1) * 64)
            mask_rows = pl.ds(pl.multiple_of(yb * 128 + half * 64, 64), 64)
            vals = [
                dl[yb * 2 + half, :, s * BLK : (s + 1) * BLK].astype(F32) for s in range(CAP)
            ]
            for b in range(NB):
                slot = slotb[b, mask_rows, :]
                out = jnp.zeros((64, 128), F32)
                for s in range(CAP):
                    out = jnp.where(slot == float(s), vals[s], out)
                lhs2[rows, b * BLK : (b + 1) * BLK] = out.astype(BF16)
        for n in range(NC):
            for q in range(CW // 256):
                part_d = lax.dot_general(
                    lhs2[...],
                    head[n * CW + q * 256 : n * CW + (q + 1) * 256, :],
                    NT,
                    preferred_element_type=F32,
                ).reshape(16, 8, 256)
                cols = slice(q * 256, (q + 1) * 256)
                if d == 0:
                    own[n * 16 : (n + 1) * 16, :, cols] = part_d
                else:
                    s2[pl.ds(n * 64 + yb * 16, 16), :, cols] = part_d.astype(BF16)
        if d > 0:
            y_in[d] = rs_y(s2, ry2, d, yb)

    gs[...] = dl[y * 2 + k0 // 2, :, CAP * BLK :].astype(F32)
    gcol = jnp.sum(
        gs[pl.ds(pl.multiple_of(((k0 % 2) * 4 + m0) * 8, 8), 8), :], axis=1, keepdims=True
    )

    def use_dnormed(n, total):
        cols = slice(n * CW, (n + 1) * CW)
        value = inv_rms * (gain_ref[:, cols] * total) - hid[:, cols] * (
            inv_rms * inv_rms * gcol / D
        )
        dhg[n * 64 + mine] = value.astype(BF16)

    rs_rest(y_in, ry2, s2a, ra2, s2b, rb2, use_dnormed)
    y_in = gather(dhg)

    ag_in = {}
    for d in order:
        yb, block = gathered(dhg, y_in, d)
        dh[pl.ds(pl.multiple_of(yb * 128, 128), 128), :] = block
        part_a = lax.dot_general(block, w[...], NT, preferred_element_type=F32)
        ags[2 * yb] = part_a[:64]
        ags[2 * yb + 1] = part_a[64:]
    agb = agr.at[pl.ds(0, 8)]
    for i in range(8):
        agb[i] = ags[i].astype(BF16)
    for d in (4, 3, 5, 2, 6, 1, 7):
        ag_in[d] = rcopy(agr.at[(t + d) % 8], agr.at[8 + d], dev_t(d))
    dg_ref[...] = jnp.dot(actt[...], dh[...], preferred_element_type=F32).astype(BF16)
    for copy in loss_in:
        copy.wait_recv()
    objective = los[0]
    for i in range(1, 8):
        objective = objective + los[i]
    loss_ref[...] = -objective / length_sum.astype(F32)
    total = ags[t]
    for d in range(1, 8):
        ag_in[d].wait_recv()
        total = total + agr[8 + d].astype(F32)
    ag_ref[...] = total.astype(BF16)
    for copy in sends:
        copy.wait_send()


def body(
    residual,
    activation,
    down_weight,
    norm_gain,
    head_weight,
    allowed,
    tokens,
    lengths,
    advantage_code,
):
    any_spec = pl.BlockSpec(memory_space=pl.ANY)
    vmem = pl.BlockSpec(memory_space=pltpu.VMEM)
    smem = pl.BlockSpec(memory_space=pltpu.SMEM)
    v = pltpu.VMEM
    loss, dg, ag = pl.pallas_call(
        kernel,
        out_shape=(
            jax.ShapeDtypeStruct((8, 128), F32),
            jax.ShapeDtypeStruct((256, 1024), BF16),
            jax.ShapeDtypeStruct((64, 256), BF16),
        ),
        in_specs=[any_spec, any_spec, any_spec, vmem, any_spec, vmem, vmem, smem, smem],
        out_specs=(vmem, vmem, vmem),
        scratch_shapes=[
            v((8, 1024), BF16),
            v((8, 64, 256), BF16),
            v((256, 512), BF16),
            v((256, 1024), BF16),
            v((1024, 1280), BF16),
            v((NB, 512, 128), F32),
            v((NC * 16, 8, CW), F32),
            v((NC * 64, 8, CW), BF16),
            v((3 * NC * 16, 8, CW), BF16),
            v((NC * 16, 8, CW), F32),
            v((NC * 16, 8, CW), BF16),
            v((3 * NC * 4, 8, CW), BF16),
            v((NC * 4, 8, CW), F32),
            v((NC * 4, 8, CW), BF16),
            v((3 * NC, 8, CW), BF16),
            v((8, 1024), F32),
            v((8, 8, 128), F32),
            v((NC * 64, 8, CW), BF16),
            v((NC * 64, 8, CW), BF16),
            v((3 * NC * 16, 8, CW), BF16),
            v((NC * 16, 8, CW), BF16),
            v((3 * NC * 4, 8, CW), BF16),
            v((NC * 4, 8, CW), BF16),
            v((3 * NC, 8, CW), BF16),
            v((NC * 64, 8, CW), BF16),
            v((128, 1024), BF16),
            v((128, 1280), F32),
            v((4, 64, CAP * BLK), F32),
            v((4, 64, CAP * BLK), F32),
            v((4, 64, CAP * BLK), F32),
            v((3, 64, CAP * BLK), F32),
            v((64, CAP * BLK), F32),
            v((NZ, 8, 128), F32),
            v((NY, 8, 128), F32),
            v((8, 64, DW), BF16),
            v((64, 128), F32),
            v((128, 1280), BF16),
            v((512, 1024), BF16),
            v((8, 64, 256), F32),
            v((16, 64, 256), BF16),
            v((8, 8, 128), F32),
            pltpu.SemaphoreType.DMA((4,)),
            pltpu.SemaphoreType.DMA((N_SEND,)),
            pltpu.SemaphoreType.DMA((N_SEND,)),
        ],
        compiler_params=pltpu.CompilerParams(
            collective_id=0, has_side_effects=True, vmem_limit_bytes=60 * 1024 * 1024
        ),
        name="step",
    )(
        residual.reshape(64, 8, 1024),
        activation,
        down_weight,
        norm_gain.reshape(1, 1024),
        head_weight,
        allowed,
        jnp.pad(tokens.reshape(1, 64), ((0, 0), (0, 64))),
        lengths,
        advantage_code,
    )
    return loss[0, 0], dg, ag


def solution(mesh):
    in_specs = (
        P(None, "tp"),
        P("tp", "vocab"),
        P("vocab", "tp"),
        P("tp"),
        P("tp", "vocab"),
        P(),
        P("tp"),
        P(),
        P(),
    )
    out_specs = (P(), P("vocab", "tp"), P("tp", "vocab"))
    return jax.shard_map(body, mesh=mesh, in_specs=in_specs, out_specs=out_specs, check_vma=False)
```

time: 1020 us -> 170 us (0.17)
  waiting for transfers between devices: 676 us -> 0 us
  blocking collectives: 291 us -> 0 us
  Pallas kernels: 0 us -> 161 us
  between operations: 16.4 us -> 0.64 us
  other arithmetic: 15.4 us -> 0 us
  matrix products: 14.9 us -> 0 us
    psum x2 -> x0, waiting for transfers between devices: 541 us -> none  [the longest x1 271 us: body(): dnormed = lax.psum(dnormed_term, 'vocab')]
    pallas_call x0 -> x1, Pallas kernels: none -> 161 us  [body(): pl.pallas_call(kernel, out_shape=(jax.ShapeDtypeStruct((8, 128), F32), ja...]
    psum x3 -> x0, blocking collectives: 155 us -> none  [the longest x1 111 us: body(): exp_total, target = lax.psum((local_total, local_target), 'vocab')]
    pmax x1 -> x0, blocking collectives: 116 us -> none  [body(): row_peak = lax.pmax(local_peak, 'vocab')]
    all_gather x1 -> x0, waiting for transfers between devices: 77.1 us -> none  [body(): dense_piece = lax.all_gather(dlogits, 'tp', axis=0, tiled=True)]
    reduce_scatter x2 -> x0, waiting for transfers between devices: 57.9 us -> none  [the longest x1 32.3 us: body(): lax.psum_scatter(jnp.dot(rows_in, head_weight, preferred_element_type=jnp...]
    all_gather x1 -> x0, blocking collectives: 19.9 us -> none  [body(): activation_rows = lax.all_gather(activation, 'tp', axis=0, tiled=True)]
    dot_general x5 -> x0, matrix products: 14.9 us -> none  [the longest x1 4.93 us: body(): jnp.dot(rows_in, head_weight, preferred_element_type=jnp.float32)]
  transfers between devices with their start and end apart: 5 -> 0, of which waited for: 5 -> 0; matrix products, arithmetic and copies ran while one was open for 0% -> 0% of each run, Pallas kernels for 0% -> 0%
where the time goes in v1:
time: 170 us; the launch traced here: 169 us
  Pallas kernels  161 us (95%)
  local copies, waits for them, and re-layouts  7.27 us (4%)
    pallas_call x1, Pallas kernels, body(): pl.pallas_call(kernel, out_shape=(jax.ShapeDtypeStruct((8, 128), F32), ja...  161 us
    unnamed x3, local copies, waits for them, and re-layouts  4.92 us

profile of v1, /device:TPU:1, one launch (start us, length us, event | category | flops | bytes accessed | tf_op | source)
XLA Modules:
  0.0 169.3 jit_solution(13345433676936982442)
XLA Ops:
  0.6 1.2 pad.4.tok_ref
  1.8 1.7 copy.12.allowed_ref
  3.5 161.4 %step.1 = (f32[8,128]{1,0:T(8,128)}, bf16[256,1024]{1,0:T(8,128)(2,1)}, bf16[64,256]{1,0:T(8,128)(2,1)}) custom-call(bf16[64,8,1024]{2,1,0:T(8,128)(2,1)} %bitcast.4, bf16[64,256]{1,0:T(8,128)(2,1)} %act_hbm.1, bf16[256,1024]{1,0:T(8,128)(2,1)} %w_hbm.1, f32[1,1024]{1,0:T(1,128)} %bitcast.5, bf16[1024,1280]{1,0:T(8,128)(2,1)} %head_hbm.1, ...), custom_call_target="tpu_custom_call" | custom-call | tf_op jit(solution)/shard_map/step/pallas_call | solution.py:548
  164.9 1.2 slice.3
  166.1 1.9 %copy.15 = bf16[256,1024]{1,0:T(8,128)(2,1)} copy(bf16[256,1024]{1,0:T(8,128)(2,1)} %get-tuple-element.13) | data formatting | bytes 1048576
  167.9 1.4 copy.16

commit v2 on v1

--- a/solution.py
+++ b/solution.py
@@ -18,8 +18,7 @@
 NEG = -1e30
 NC = 2
 CW = 1024 // NC
-DW = CAP * BLK + BLK
-N_SEND = 200
+N_SEND = 240
 NT = (((1,), (1,)), ((), ()))
 
 
@@ -33,18 +32,21 @@
     tok_ref,
     len_ref,
     adv_ref,
+    actt,
+    dh,
+    ag_ref,
     loss_ref,
-    dg_ref,
-    ag_ref,
     res,
     act,
-    actt,
     w,
     head,
     slotb,
     own,
+    fo,
     s1,
-    ry1,
+    f1,
+    rp1,
+    rm1,
     t1,
     s1a,
     ra1,
@@ -53,9 +55,13 @@
     rb1,
     hid,
     ssq,
+    iv,
+    ivy,
     nrm,
     s2,
-    ry2,
+    f2,
+    rp2,
+    rm2,
     s2a,
     ra2,
     s2b,
@@ -71,9 +77,8 @@
     stz,
     sty,
     dl,
-    gs,
+    gv,
     lhs2,
-    dh,
     ags,
     agr,
     los,
@@ -108,7 +113,7 @@
     peers = (
         [dev_t(d) for d in range(1, 8)]
         + [dev_y(d) for d in range(1, 4)]
-        + [dev_z(d) for d in (1, 2, 4, 8, 12, 14, 15)]
+        + [dev_z(d) for d in range(1, NZ)]
     )
     for dev in peers:
         pl.semaphore_signal(barrier, inc=1, device_id=dev, device_id_type=MESH)
@@ -126,15 +131,18 @@
 
     def prep(i, carry):
         rows = pl.ds(pl.multiple_of(i * 128, 128), 128)
-        listed = allowed_ref[rows, :]
-        run = jnp.zeros((128, 1), F32)
+        listed = allowed_ref[:, rows]
+        run = jnp.zeros((1, 128), F32)
+        slots = []
         for b in range(NB):
             hit = jnp.max(
-                jnp.where(listed == first_block + b, 1.0, 0.0).astype(F32), axis=1, keepdims=True
+                jnp.where(listed == first_block + b, 1.0, 0.0).astype(F32), axis=0, keepdims=True
             )
-            slot = jnp.where(hit > 0.5, run, 99.0)
+            slots.append(jnp.where(hit > 0.5, run, 99.0))
             run = run + hit
-            slotb[b, rows, :] = jnp.broadcast_to(slot, (128, 128))
+        turned = jnp.concatenate(slots + [jnp.zeros((128 - NB, 128), F32)], axis=0).T
+        for b in range(NB):
+            slotb[b, rows, :] = jnp.broadcast_to(turned[:, b : b + 1], (128, 128))
         return carry
 
     lax.fori_loop(0, 4, prep, 0)
@@ -157,40 +165,79 @@
         sends.append(copy)
         return copy
 
+    def reserve(k):
+        i = count[0]
+        count[0] += k
+        return i
+
+    def described(src, dst, dev, i):
+        return pltpu.make_async_remote_copy(
+            src_ref=src,
+            dst_ref=dst,
+            send_sem=ssem.at[i],
+            recv_sem=rsem.at[i],
+            device_id=dev,
+            device_id_type=MESH,
+        )
+
     loads[0].wait()
     pl.semaphore_wait(barrier, len(peers))
 
-    a_in = {}
-    for d in (4, 3, 5, 2, 6, 1, 7):
-        a_in[d] = rcopy(act.at[t], act.at[t], dev_t(d))
+    a_in = [rcopy(act.at[t], act.at[t], dev_t(d)) for d in (4, 3, 5, 2, 6, 1, 7)]
     loads[1].wait()
-    for d in range(1, 8):
-        a_in[d].wait_recv()
+    for copy in a_in:
+        copy.wait_recv()
 
     def act_rows(yb):
         return jnp.concatenate([act[2 * yb], act[2 * yb + 1]], axis=0)
 
-    def rs_y(s, ry, d, yb):
-        return [
-            rcopy(
-                s.at[pl.ds(n * 64 + yb * 16, 16)],
-                ry.at[pl.ds(((d - 1) * NC + n) * 16, 16)],
-                dev_y(d),
+    def part16(n, k=16):
+        return slice(n * k, (n + 1) * k)
+
+    def rs_start(block, s, f, rp, rm):
+        step_one, step_two = {}, {}
+        far = (y + 2) % 4
+        block(far, lambda n, cols, part: s.__setitem__(
+            (pl.ds(n * 64 + far * 16, 16), slice(None), cols), part.astype(BF16)))
+        for n in range(NC):
+            step_one[n] = rcopy(
+                s.at[pl.ds(n * 64 + far * 16, 16)], f.at[pl.ds(n * 16, 16)], dev_y(1 if n % 2 == 0 else 3)
             )
-            for n in range(NC)
-        ]
-
-    def rs_rest(y_in, ry, sa, ra, sb, rb, use):
+        for d, dst in ((1, rp), (3, rm)):
+            yb = (y + d) % 4
+
+            def put(n, cols, part, d=d, yb=yb):
+                if (n % 2 == 0) == (d == 1):
+                    fo[part16(n), :, cols] = part
+                else:
+                    s[pl.ds(n * 64 + yb * 16, 16), :, cols] = part.astype(BF16)
+
+            block(yb, put)
+            for n in range(NC):
+                if (n % 2 == 0) != (d == 1):
+                    rows = pl.ds(n * 64 + yb * 16, 16)
+                    step_two[d, n] = rcopy(s.at[rows], dst.at[pl.ds(n * 16, 16)], dev_y(d))
+        for n in range(NC):
+            d, dst = ((1, rp), (3, rm))[n % 2]
+            rows = pl.ds(n * 64 + ((y + d) % 4) * 16, 16)
+            step_one[n].wait_recv()
+            s[rows] = (fo[part16(n)] + f[part16(n)].astype(F32)).astype(BF16)
+            step_two[d, n] = rcopy(s.at[rows], dst.at[pl.ds(n * 16, 16)], dev_y(d))
+
+        def put_own(n, cols, part):
+            own[part16(n), :, cols] = part
+
+        block(y, put_own)
+        return step_two
+
+    def rs_rest(y_in, rp, rm, sa, ra, sb, rb, use):
         a_in, b_in = [], []
         for n in range(NC):
-            total = own[n * 16 : (n + 1) * 16]
-            for d in (1, 3, 2):
-                y_in[d][n].wait_recv()
-            for d in (1, 3, 2):
-                q = (d - 1) * NC + n
-                total = total + ry[q * 16 : (q + 1) * 16].astype(F32)
-            t1[n * 16 : (n + 1) * 16] = total
-            sa[n * 16 : (n + 1) * 16] = total.astype(BF16)
+            for d in (1, 3):
+                y_in[d, n].wait_recv()
+            total = own[part16(n)] + rp[part16(n)].astype(F32) + rm[part16(n)].astype(F32)
+            t1[part16(n)] = total
+            sa[part16(n)] = total.astype(BF16)
             far = 2 if n % 2 == 0 else 14
             a_in.append(
                 [
@@ -207,10 +254,9 @@
                 copy.wait_recv()
             total = t1[pl.ds(n * 16 + k0 * 4, 4)]
             for j in range(3):
-                q = j * NC + n
-                total = total + ra[q * 4 : (q + 1) * 4].astype(F32)
-            t1a[n * 4 : (n + 1) * 4] = total
-            sb[n * 4 : (n + 1) * 4] = total.astype(BF16)
+                total = total + ra[part16(j * NC + n, 4)].astype(F32)
+            t1a[part16(n, 4)] = total
+            sb[part16(n, 4)] = total.astype(BF16)
             b_in.append(
                 [
                     rcopy(
@@ -229,36 +275,53 @@
                 total = total + rb[dm * NC + n].astype(F32)
             use(n, total)
 
-    def gather(g):
-        base = y * 16
-        b_in, y_in = [], []
-
-        def to_y(n, cls):
-            rows = pl.ds(n * 64 + base + cls * 4, 4)
-            return {d: rcopy(g.at[rows], g.at[rows], dev_y(d)) for d in (2, 1, 3)}
-
-        for n in range(NC):
-            row = pl.ds(n * 64 + base + k0 * 4 + m0, 1)
+    def to_y(g, n, cls):
+        rows = pl.ds(n * 64 + y * 16 + cls * 4, 4)
+        return {d: rcopy(g.at[rows], g.at[rows], dev_y(d)) for d in (1, 3)}
+
+    def gather_start(g):
+        b_in = []
+        for n in range(NC):
+            row = pl.ds(n * 64 + y * 16 + k0 * 4 + m0, 1)
             b_in.append([rcopy(g.at[row], g.at[row], dev_z(4 * dm)) for dm in (2, 1, 3)])
-        a_in = []
+        return b_in
+
+    def gather_rest(g, b_in):
+        a_in, y_in = [], []
         for n in range(NC):
             for copy in b_in[n]:
                 copy.wait_recv()
-            rows = pl.ds(n * 64 + base + k0 * 4, 4)
+            rows = pl.ds(n * 64 + y * 16 + k0 * 4, 4)
             far = 2 if n % 2 == 0 else 14
             a_in.append([rcopy(g.at[rows], g.at[rows], dev_z(dz)) for dz in (far, 1, 15)])
-            y_in.append([to_y(n, k0)])
-        for n in range(NC):
-            for j, dk in ((1, 3), (2, 1), (0, 2)):
+            y_in.append([to_y(g, n, k0)])
+        for j, dk in ((1, 3), (2, 1), (0, 2)):
+            for n in range(NC):
                 a_in[n][j].wait_recv()
-                y_in[n].append(to_y(n, (k0 + dk) % 4))
+                y_in[n].append(to_y(g, n, (k0 + dk) % 4))
         return y_in
 
-    def gathered(g, y_in, d):
-        if d > 0:
+    def gather_forward(g, y_in):
+        far_in = []
+        for j, dk in enumerate((0, 3, 1, 2)):
             for n in range(NC):
-                for part in y_in[n]:
-                    part[d].wait_recv()
+                d = 1 if n % 2 == 0 else 3
+                y_in[n][j][d].wait_recv()
+                rows = pl.ds(n * 64 + ((y + 4 - d) % 4) * 16 + ((k0 + dk) % 4) * 4, 4)
+                far_in.append(rcopy(g.at[rows], g.at[rows], dev_y(d)))
+        return far_in
+
+    def gather_wait(y_in, far_in, d):
+        if d == 2:
+            for copy in far_in:
+                copy.wait_recv()
+        elif d > 0:
+            for n in range(NC):
+                if (n % 2 == 0) != (d == 1):
+                    for part in y_in[n]:
+                        part[d].wait_recv()
+
+    def gathered(g, d):
         yb = (y + 4 - d) % 4
         pieces = [
             g[pl.ds(n * 64 + yb * 16, 16)].astype(F32).reshape(128, CW).astype(BF16)
@@ -266,19 +329,12 @@
         ]
         return yb, jnp.concatenate(pieces, axis=1)
 
-    y_in = {}
-    for d in (2, 1, 3, 0):
-        yb = (y + d) % 4
+    def down_block(yb, put):
         for n in range(NC):
             part = jnp.dot(act_rows(yb), w[:, n * CW : (n + 1) * CW], preferred_element_type=F32)
-            part = part.reshape(16, 8, CW)
-            if d == 0:
-                own[n * 16 : (n + 1) * 16] = part
-            else:
-                s1[pl.ds(n * 64 + yb * 16, 16)] = part.astype(BF16)
-        if d > 0:
-            y_in[d] = rs_y(s1, ry1, d, yb)
-
+            put(n, slice(None), part.reshape(16, 8, CW))
+
+    y_in = rs_start(down_block, s1, f1, rp1, rm1)
     for i in range(8):
         actt[:, i * 64 : (i + 1) * 64] = act[i].astype(F32).T.astype(BF16)
     loads[2].wait()
@@ -286,8 +342,13 @@
     def use_hidden(n, total):
         hid[:, n * CW : (n + 1) * CW] = res[:, n * CW : (n + 1) * CW].astype(F32) + total
 
-    rs_rest(y_in, ry1, s1a, ra1, s1b, rb1, use_hidden)
-
+    rs_rest(y_in, rp1, rm1, s1a, ra1, s1b, rb1, use_hidden)
+
+    mine = y * 16 + k0 * 4 + m0
+    for n in range(NC):
+        cols = slice(n * CW, (n + 1) * CW)
+        nrm[n * 64 + mine] = (hid[:, cols] * gain_ref[:, cols]).astype(BF16)
+    nrm_in = gather_start(nrm)
     h = hid[...]
     ssq[t] = jnp.broadcast_to(jnp.sum(h * h, axis=1, keepdims=True), (8, 128))
     ss_in = [rcopy(ssq.at[t], ssq.at[t], dev_t(d)) for d in (4, 3, 5, 2, 6, 1, 7)]
@@ -296,19 +357,43 @@
     square = ssq[0]
     for i in range(1, 8):
         square = square + ssq[i]
-    inv_rms = lax.rsqrt(square[:, :1] / D + 1e-06)
-    mine = y * 16 + k0 * 4 + m0
-    for n in range(NC):
-        cols = slice(n * CW, (n + 1) * CW)
-        nrm[n * 64 + mine] = (hid[:, cols] * inv_rms * gain_ref[:, cols]).astype(BF16)
-    y_in = gather(nrm)
+    inv_rms = lax.rsqrt(square / D + 1e-06)
+    spot = lax.broadcasted_iota(jnp.int32, (8, 128), 1) == (
+        lax.broadcasted_iota(jnp.int32, (8, 128), 0) + (k0 * 4 + m0) * 8
+    )
+    iv[z] = jnp.sum(jnp.where(spot, inv_rms, 0.0), axis=0, keepdims=True)
+    inv_rms = inv_rms[:, :1]
+    iv_in = [rcopy(iv.at[z], iv.at[z], dev_z(d)) for d in (8, 7, 9, 6, 10, 5, 11, 4, 12, 3, 13, 2, 14, 1, 15)]
+    y_in = gather_rest(nrm, nrm_in)
+    for copy in iv_in:
+        copy.wait_recv()
+    inv_row = iv[0]
+    for i in range(1, NZ):
+        inv_row = inv_row + iv[i]
+    ivy[y] = inv_row
+    ivy_in = [rcopy(ivy.at[y], ivy.at[y], dev_y(d)) for d in (2, 1, 3)]
     loads[3].wait()
 
-    x_in = {}
     order = (0, 1, 3, 2)
+    lx_at = reserve(4)
     p_in = []
+    def x_copy(dx):
+        return described(lx.at[(x + dx) % 4], lxr.at[dx], dev_x(dx), lx_at + dx)
+
+    def combine(copy, row_block):
+        copy.wait_recv()
+        lx[row_block] = lx[row_block] + lpr[row_block]
+        dx = (row_block + 4 - x) % 4
+
+        @pl.when(dx != 0)
+        def _():
+            x_copy(dx).start()
+
+    far_in = None
+    blocks = []
     for d in order:
-        yb, block = gathered(nrm, y_in, d)
+        gather_wait(y_in, far_in, d)
+        yb, block = gathered(nrm, d)
         lhs[...] = block
 
         def columns(j, carry):
@@ -333,21 +418,28 @@
         compact(1 - c, lp.at[yb])
         p_in.append(rcopy(lp.at[yb], lpr.at[yb], partner))
         compact(c, lx.at[yb])
-        if d != order[0]:
-            combine(p_prev, yb_prev)
-        p_prev, yb_prev = p_in[-1], yb
-
-        def combine(copy, row_block):
-            copy.wait_recv()
-            lx[row_block] = lx[row_block] + lpr[row_block]
-
-    combine(p_prev, yb_prev)
-    x_in = {d: rcopy(lx.at[(x + d) % 4], lxr.at[d - 1], dev_x(d)) for d in (2, 1, 3)}
+        blocks.append(yb)
+        if d == 0:
+            far_in = gather_forward(nrm, y_in)
+        if d != 1:
+            while blocks:
+                combine(p_in[-len(blocks)], blocks[0])
+                blocks = blocks[1:]
+
+    for copy in ivy_in:
+        copy.wait_recv()
+    scale_row = ivy[t // 2]
+    turned = lax.broadcasted_iota(jnp.int32, (64, 128), 1) == (
+        lax.broadcasted_iota(jnp.int32, (64, 128), 0) + c * 64
+    )
+    scale = jnp.sum(jnp.where(turned, scale_row, 0.0), axis=1, keepdims=True)
     total = lx[x]
-    for d in (1, 3, 2):
-        x_in[d].wait_recv()
-        total = total + lxr[d - 1]
-    lg[...] = total
+    for dx in (1, 3, 2):
+        x_copy(dx).wait_recv()
+        total = total + lxr[dx]
+    for dx in (1, 3, 2):
+        x_copy(dx).wait_send()
+    lg[...] = total * scale
 
     own_rows = pl.ds(pl.multiple_of(t * 64, 64), 64)
     lane = lax.broadcasted_iota(jnp.int32, (64, 128), 1)
@@ -359,7 +451,11 @@
     def to_col(row):
         return jnp.sum(jnp.where(eye, row, 0.0), axis=1, keepdims=True)
 
-    tok = to_col(tok_ref[...].astype(F32)).astype(jnp.int32)
+    small_eye = lax.broadcasted_iota(jnp.int32, (64, 64), 0) == lax.broadcasted_iota(
+        jnp.int32, (64, 64), 1
+    )
+    tok = jnp.sum(jnp.where(small_eye, tok_ref[...].astype(F32), 0.0), axis=1, keepdims=True)
+    tok = tok.astype(jnp.int32)
     tok_block = (tok >> 7) - first_block
     tok_lane = tok & 127
     seen = jnp.zeros((64, 128), F32)
@@ -386,16 +482,12 @@
     tot = jnp.sum(tot, axis=1, keepdims=True)
     mom = jnp.sum(mom, axis=1, keepdims=True)
     tgt = jnp.sum(tgt, axis=1, keepdims=True)
-    at = k0 * 4 + m0
-    stz[at] = jnp.concatenate(
-        [to_row(peak), to_row(tot), to_row(mom), to_row(tgt), jnp.zeros((4, 128), F32)], axis=0
-    )
-    b_in = [rcopy(stz.at[at], stz.at[at], dev_z(4 * dm)) for dm in (2, 1, 3)]
-    for copy in b_in:
-        copy.wait_recv()
-    rows = pl.ds(k0 * 4, 4)
-    a_in = [rcopy(stz.at[rows], stz.at[rows], dev_z(dz)) for dz in (2, 1, 15)]
-    for copy in a_in:
+    stz[z] = jnp.concatenate([to_row(peak), to_row(tot), to_row(mom), to_row(tgt)], axis=0)
+    st_in = [
+        rcopy(stz.at[z], stz.at[z], dev_z(d))
+        for d in (8, 7, 9, 6, 10, 5, 11, 4, 12, 3, 13, 2, 14, 1, 15)
+    ]
+    for copy in st_in:
         copy.wait_recv()
 
     def join(parts):
@@ -414,7 +506,7 @@
         return top, tot, mom, tgt
 
     top, tot, mom, tgt = join([stz[i] for i in range(NZ)])
-    sty[y] = jnp.concatenate([top, tot, mom, tgt, jnp.zeros((4, 128), F32)], axis=0)
+    sty[y] = jnp.concatenate([top, tot, mom, tgt], axis=0)
     y_st = [rcopy(sty.at[y], sty.at[y], dev_y(d)) for d in (2, 1, 3)]
     for copy in y_st:
         copy.wait_recv()
@@ -439,26 +531,20 @@
         prob = jnp.where(seen > float(s), jnp.exp(val - top), 0.0) / tot
         hot = jnp.where((tok_slot == float(s)) & (lane == tok_lane), 1.0, 0.0)
         dl[t, :, s * BLK : (s + 1) * BLK] = (weight * (prob - hot)).astype(BF16)
-    g_hi = gdot.astype(BF16).astype(F32)
-    g_mid = (gdot - g_hi).astype(BF16).astype(F32)
-    g_lo = gdot - g_hi - g_mid
-    tail = jnp.where(lane == 0, g_hi, jnp.where(lane == 1, g_mid, jnp.where(lane == 2, g_lo, 0.0)))
-    dl[t, :, CAP * BLK :] = tail.astype(BF16)
-
     dx_in = {d: rcopy(dl.at[t], dl.at[t], dev_x(d)) for d in (2, 1, 3)}
     d_in = {0: rcopy(dl.at[t], dl.at[t], partner)}
+    gv[t] = to_row(gdot)
+    g_in = [rcopy(gv.at[t], gv.at[t], dev_t(d)) for d in (4, 3, 5, 2, 6, 1, 7)]
+    los[t] = jnp.broadcast_to(part, (8, 128))
+    loss_in = [rcopy(los.at[t], los.at[t], dev_t(d)) for d in range(1, 8)]
     for d in (1, 3, 2):
         dx_in[d].wait_recv()
         slot = ((x + 4 - d) % 4) * 2 + c
         d_in[d] = rcopy(dl.at[slot], dl.at[slot], partner)
-    los[t] = jnp.broadcast_to(part, (8, 128))
-    loss_in = [rcopy(los.at[t], los.at[t], dev_t(d)) for d in range(1, 8)]
     for d in range(4):
         d_in[d].wait_recv()
 
-    y_in = {}
-    for d in (2, 1, 3, 0):
-        yb = (y + d) % 4
+    def head_block(yb, put):
         for half in range(2):
             rows = slice(half * 64, (half + 1) * 64)
             mask_rows = pl.ds(pl.multiple_of(yb * 128 + half * 64, 64), 64)
@@ -473,24 +559,21 @@
                 lhs2[rows, b * BLK : (b + 1) * BLK] = out.astype(BF16)
         for n in range(NC):
             for q in range(CW // 256):
-                part_d = lax.dot_general(
+                part = lax.dot_general(
                     lhs2[...],
                     head[n * CW + q * 256 : n * CW + (q + 1) * 256, :],
                     NT,
                     preferred_element_type=F32,
-                ).reshape(16, 8, 256)
-                cols = slice(q * 256, (q + 1) * 256)
-                if d == 0:
-                    own[n * 16 : (n + 1) * 16, :, cols] = part_d
-                else:
-                    s2[pl.ds(n * 64 + yb * 16, 16), :, cols] = part_d.astype(BF16)
-        if d > 0:
-            y_in[d] = rs_y(s2, ry2, d, yb)
-
-    gs[...] = dl[y * 2 + k0 // 2, :, CAP * BLK :].astype(F32)
-    gcol = jnp.sum(
-        gs[pl.ds(pl.multiple_of(((k0 % 2) * 4 + m0) * 8, 8), 8), :], axis=1, keepdims=True
+                )
+                put(n, slice(q * 256, (q + 1) * 256), part.reshape(16, 8, 256))
+
+    y_in = rs_start(head_block, s2, f2, rp2, rm2)
+    for copy in g_in:
+        copy.wait_recv()
+    spot = lax.broadcasted_iota(jnp.int32, (8, 128), 1) == (
+        lax.broadcasted_iota(jnp.int32, (8, 128), 0) + ((k0 % 2) * 4 + m0) * 8
     )
+    gcol = jnp.sum(jnp.where(spot, gv[y * 2 + k0 // 2], 0.0), axis=1, keepdims=True)
 
     def use_dnormed(n, total):
         cols = slice(n * CW, (n + 1) * CW)
@@ -499,22 +582,24 @@
         )
         dhg[n * 64 + mine] = value.astype(BF16)
 
-    rs_rest(y_in, ry2, s2a, ra2, s2b, rb2, use_dnormed)
-    y_in = gather(dhg)
+    rs_rest(y_in, rp2, rm2, s2a, ra2, s2b, rb2, use_dnormed)
+    y_in = gather_rest(dhg, gather_start(dhg))
 
     ag_in = {}
+    far_in = None
     for d in order:
-        yb, block = gathered(dhg, y_in, d)
+        gather_wait(y_in, far_in, d)
+        yb, block = gathered(dhg, d)
         dh[pl.ds(pl.multiple_of(yb * 128, 128), 128), :] = block
         part_a = lax.dot_general(block, w[...], NT, preferred_element_type=F32)
         ags[2 * yb] = part_a[:64]
         ags[2 * yb + 1] = part_a[64:]
-    agb = agr.at[pl.ds(0, 8)]
-    for i in range(8):
-        agb[i] = ags[i].astype(BF16)
+        agr[2 * yb] = part_a[:64].astype(BF16)
+        agr[2 * yb + 1] = part_a[64:].astype(BF16)
+        if d == order[0]:
+            far_in = gather_forward(dhg, y_in)
     for d in (4, 3, 5, 2, 6, 1, 7):
         ag_in[d] = rcopy(agr.at[(t + d) % 8], agr.at[8 + d], dev_t(d))
-    dg_ref[...] = jnp.dot(actt[...], dh[...], preferred_element_type=F32).astype(BF16)
     for copy in loss_in:
         copy.wait_recv()
     objective = los[0]
@@ -528,6 +613,12 @@
     ag_ref[...] = total.astype(BF16)
     for copy in sends:
         copy.wait_send()
+
+
+def last(actt, dh, ag, loss, loss_ref, dg_ref, ag_ref):
+    dg_ref[...] = jnp.dot(actt[...], dh[...], preferred_element_type=F32).astype(BF16)
+    ag_ref[...] = ag[...]
+    loss_ref[...] = loss[0:1, 0:1]
 
 
 def body(
@@ -545,25 +636,28 @@
     vmem = pl.BlockSpec(memory_space=pltpu.VMEM)
     smem = pl.BlockSpec(memory_space=pltpu.SMEM)
     v = pltpu.VMEM
-    loss, dg, ag = pl.pallas_call(
+    out = pl.pallas_call(
         kernel,
         out_shape=(
+            jax.ShapeDtypeStruct((256, 512), BF16),
+            jax.ShapeDtypeStruct((512, 1024), BF16),
+            jax.ShapeDtypeStruct((64, 256), BF16),
             jax.ShapeDtypeStruct((8, 128), F32),
-            jax.ShapeDtypeStruct((256, 1024), BF16),
-            jax.ShapeDtypeStruct((64, 256), BF16),
         ),
         in_specs=[any_spec, any_spec, any_spec, vmem, any_spec, vmem, vmem, smem, smem],
-        out_specs=(vmem, vmem, vmem),
+        out_specs=(vmem, vmem, vmem, vmem),
         scratch_shapes=[
             v((8, 1024), BF16),
             v((8, 64, 256), BF16),
-            v((256, 512), BF16),
             v((256, 1024), BF16),
             v((1024, 1280), BF16),
             v((NB, 512, 128), F32),
             v((NC * 16, 8, CW), F32),
+            v((NC * 16, 8, CW), F32),
             v((NC * 64, 8, CW), BF16),
-            v((3 * NC * 16, 8, CW), BF16),
+            v((NC * 16, 8, CW), BF16),
+            v((NC * 16, 8, CW), BF16),
+            v((NC * 16, 8, CW), BF16),
             v((NC * 16, 8, CW), F32),
             v((NC * 16, 8, CW), BF16),
             v((3 * NC * 4, 8, CW), BF16),
@@ -572,9 +666,13 @@
             v((3 * NC, 8, CW), BF16),
             v((8, 1024), F32),
             v((8, 8, 128), F32),
+            v((NZ, 1, 128), F32),
+            v((NY, 1, 128), F32),
             v((NC * 64, 8, CW), BF16),
             v((NC * 64, 8, CW), BF16),
-            v((3 * NC * 16, 8, CW), BF16),
+            v((NC * 16, 8, CW), BF16),
+            v((NC * 16, 8, CW), BF16),
+            v((NC * 16, 8, CW), BF16),
             v((NC * 16, 8, CW), BF16),
             v((3 * NC * 4, 8, CW), BF16),
             v((NC * 4, 8, CW), BF16),
@@ -585,14 +683,13 @@
             v((4, 64, CAP * BLK), F32),
             v((4, 64, CAP * BLK), F32),
             v((4, 64, CAP * BLK), F32),
-            v((3, 64, CAP * BLK), F32),
+            v((4, 64, CAP * BLK), F32),
             v((64, CAP * BLK), F32),
-            v((NZ, 8, 128), F32),
-            v((NY, 8, 128), F32),
-            v((8, 64, DW), BF16),
-            v((64, 128), F32),
+            v((NZ, 4, 128), F32),
+            v((NY, 4, 128), F32),
+            v((8, 64, CAP * BLK), BF16),
+            v((8, 1, 128), F32),
             v((128, 1280), BF16),
-            v((512, 1024), BF16),
             v((8, 64, 256), F32),
             v((16, 64, 256), BF16),
             v((8, 8, 128), F32),
@@ -610,12 +707,23 @@
         down_weight,
         norm_gain.reshape(1, 1024),
         head_weight,
-        allowed,
-        jnp.pad(tokens.reshape(1, 64), ((0, 0), (0, 64))),
+        allowed.T,
+        tokens.reshape(1, 64),
         lengths,
         advantage_code,
     )
-    return loss[0, 0], dg, ag
+    loss, dg, ag = pl.pallas_call(
+        last,
+        out_shape=(
+            jax.ShapeDtypeStruct((1, 1), F32),
+            jax.ShapeDtypeStruct((256, 1024), BF16),
+            jax.ShapeDtypeStruct((64, 256), BF16),
+        ),
+        in_specs=[vmem] * 4,
+        out_specs=(vmem, vmem, vmem),
+        name="last",
+    )(*out)
+    return loss.reshape(()), dg, ag
 
 
 def solution(mesh):

time: 170 us -> 150 us (0.88)
  Pallas kernels: 161 us -> 149 us
  local copies, waits for them, and re-layouts: 7.27 us -> 0 us
    pallas_call x1 -> x2, Pallas kernels: 161 us -> 149 us  [the longest x1 146 us: body(): pl.pallas_call(kernel, out_shape=(jax.ShapeDtypeStruct((256, 512), BF16),...]
    unnamed x3 -> x0, local copies, waits for them, and re-layouts: 4.92 us -> none
where the time goes in v2:
time: 150 us; the launch traced here: 149 us
  Pallas kernels  149 us (99%)
    pallas_call x1, Pallas kernels, body(): pl.pallas_call(kernel, out_shape=(jax.ShapeDtypeStruct((256, 512), BF16),...  146 us

profile of v2, /device:TPU:1, one launch (start us, length us, event | category | flops | bytes accessed | tf_op | source)
XLA Modules:
  0.0 149.4 jit_solution(7434216507384233435)
XLA Ops:
  0.6 146.3 %step.1 = (bf16[256,512]{1,0:T(8,128)(2,1)}, bf16[512,1024]{1,0:T(8,128)(2,1)}, bf16[64,256]{1,0:T(8,128)(2,1)}, f32[8,128]{1,0:T(8,128)}) custom-call(bf16[64,8,1024]{2,1,0:T(8,128)(2,1)} %bitcast.5, bf16[64,256]{1,0:T(8,128)(2,1)} %act_hbm.1, bf16[256,1024]{1,0:T(8,128)(2,1)} %w_hbm.1, f32[1,1024]{1,0:T(1,128)} %bitcast.7, bf16[1024,1280]{1,0:T(8,128)(2,1)} %head_hbm.1, ...), custom_call_target="tpu_custom_call" | custom-call | tf_op jit(solution)/shard_map/step/pallas_call | solution.py:639
  146.9 2.5 %last.1 = (f32[1,1]{1,0:T(1,128)}, bf16[256,1024]{1,0:T(8,128)(2,1)}, bf16[64,256]{1,0:T(8,128)(2,1)}) custom-call(bf16[256,512]{1,0:T(8,128)(2,1)} %get-tuple-element.10.actt, bf16[512,1024]{1,0:T(8,128)(2,1)} %get-tuple-element.11.dh, bf16[64,256]{1,0:T(8,128)(2,1)} %get-tuple-element.12.ag, f32[8,128]{1,0:T(8,128)} %get-tuple-element.13.loss), custom_call_target="tpu_custom_call" | custom-call | tf_op jit(solution)/shard_map/last/pallas_call | solution.py:715

commit v3 on v2

--- a/solution.py
+++ b/solution.py
@@ -16,9 +16,9 @@
 NZ = 16
 NX = 4
 NEG = -1e30
-NC = 2
+NC = 4
 CW = 1024 // NC
-N_SEND = 240
+N_SEND = 330
 NT = (((1,), (1,)), ((), ()))
 
 
@@ -51,7 +51,7 @@
     s1a,
     ra1,
     t1a,
-    s1b,
+    t1b,
     rb1,
     hid,
     ssq,
@@ -201,9 +201,11 @@
             (pl.ds(n * 64 + far * 16, 16), slice(None), cols), part.astype(BF16)))
         for n in range(NC):
             step_one[n] = rcopy(
-                s.at[pl.ds(n * 64 + far * 16, 16)], f.at[pl.ds(n * 16, 16)], dev_y(1 if n % 2 == 0 else 3)
+                s.at[pl.ds(n * 64 + far * 16, 16)],
+                f.at[pl.ds(n * 16, 16)],
+                dev_y(1 if n % 2 == 0 else 3),
             )
-        for d, dst in ((1, rp), (3, rm)):
+        for d in (1, 3):
             yb = (y + d) % 4
 
             def put(n, cols, part, d=d, yb=yb):
@@ -213,24 +215,29 @@
                     s[pl.ds(n * 64 + yb * 16, 16), :, cols] = part.astype(BF16)
 
             block(yb, put)
-            for n in range(NC):
-                if (n % 2 == 0) != (d == 1):
-                    rows = pl.ds(n * 64 + yb * 16, 16)
-                    step_two[d, n] = rcopy(s.at[rows], dst.at[pl.ds(n * 16, 16)], dev_y(d))
-        for n in range(NC):
-            d, dst = ((1, rp), (3, rm))[n % 2]
-            rows = pl.ds(n * 64 + ((y + d) % 4) * 16, 16)
-            step_one[n].wait_recv()
-            s[rows] = (fo[part16(n)] + f[part16(n)].astype(F32)).astype(BF16)
-            step_two[d, n] = rcopy(s.at[rows], dst.at[pl.ds(n * 16, 16)], dev_y(d))
 
         def put_own(n, cols, part):
             own[part16(n), :, cols] = part
 
-        block(y, put_own)
+        def send(n, d):
+            rows = pl.ds(n * 64 + ((y + d) % 4) * 16, 16)
+            step_two[d, n] = rcopy(
+                s.at[rows], (rp if d == 1 else rm).at[pl.ds(n * 16, 16)], dev_y(d)
+            )
+
+        for first in range(0, NC, 2):
+            send(first, 3)
+            send(first + 1, 1)
+            if first == 0:
+                block(y, put_own)
+            for n, d in ((first, 1), (first + 1, 3)):
+                rows = pl.ds(n * 64 + ((y + d) % 4) * 16, 16)
+                step_one[n].wait_recv()
+                s[rows] = (fo[part16(n)] + f[part16(n)].astype(F32)).astype(BF16)
+                send(n, d)
         return step_two
 
-    def rs_rest(y_in, rp, rm, sa, ra, sb, rb, use):
+    def rs_rest(y_in, rp, rm, sa, ra, ta, sb, rb, use):
         a_in, b_in = [], []
         for n in range(NC):
             for d in (1, 3):
@@ -255,8 +262,9 @@
             total = t1[pl.ds(n * 16 + k0 * 4, 4)]
             for j in range(3):
                 total = total + ra[part16(j * NC + n, 4)].astype(F32)
-            t1a[part16(n, 4)] = total
-            sb[part16(n, 4)] = total.astype(BF16)
+            ta[part16(n, 4)] = total
+            if sb is not ta:
+                sb[part16(n, 4)] = total.astype(BF16)
             b_in.append(
                 [
                     rcopy(
@@ -270,64 +278,78 @@
         for n in range(NC):
             for copy in b_in[n]:
                 copy.wait_recv()
-            total = t1a[n * 4 + m0]
+            total = ta[n * 4 + m0]
             for dm in range(3):
                 total = total + rb[dm * NC + n].astype(F32)
             use(n, total)
 
-    def to_y(g, n, cls):
-        rows = pl.ds(n * 64 + y * 16 + cls * 4, 4)
-        return {d: rcopy(g.at[rows], g.at[rows], dev_y(d)) for d in (1, 3)}
-
-    def gather_start(g):
-        b_in = []
-        for n in range(NC):
-            row = pl.ds(n * 64 + y * 16 + k0 * 4 + m0, 1)
-            b_in.append([rcopy(g.at[row], g.at[row], dev_z(4 * dm)) for dm in (2, 1, 3)])
-        return b_in
-
-    def gather_rest(g, b_in):
-        a_in, y_in = [], []
-        for n in range(NC):
-            for copy in b_in[n]:
-                copy.wait_recv()
-            rows = pl.ds(n * 64 + y * 16 + k0 * 4, 4)
-            far = 2 if n % 2 == 0 else 14
-            a_in.append([rcopy(g.at[rows], g.at[rows], dev_z(dz)) for dz in (far, 1, 15)])
-            y_in.append([to_y(g, n, k0)])
-        for j, dk in ((1, 3), (2, 1), (0, 2)):
-            for n in range(NC):
-                a_in[n][j].wait_recv()
-                y_in[n].append(to_y(g, n, (k0 + dk) % 4))
-        return y_in
-
-    def gather_forward(g, y_in):
-        far_in = []
-        for j, dk in enumerate((0, 3, 1, 2)):
-            for n in range(NC):
-                d = 1 if n % 2 == 0 else 3
-                y_in[n][j][d].wait_recv()
-                rows = pl.ds(n * 64 + ((y + 4 - d) % 4) * 16 + ((k0 + dk) % 4) * 4, 4)
-                far_in.append(rcopy(g.at[rows], g.at[rows], dev_y(d)))
-        return far_in
-
-    def gather_wait(y_in, far_in, d):
-        if d == 2:
-            for copy in far_in:
-                copy.wait_recv()
-        elif d > 0:
-            for n in range(NC):
-                if (n % 2 == 0) != (d == 1):
-                    for part in y_in[n]:
-                        part[d].wait_recv()
-
-    def gathered(g, d):
-        yb = (y + 4 - d) % 4
-        pieces = [
-            g[pl.ds(n * 64 + yb * 16, 16)].astype(F32).reshape(128, CW).astype(BF16)
-            for n in range(NC)
-        ]
-        return yb, jnp.concatenate(pieces, axis=1)
+    def piece(dy, dz):
+        zz = (z + dz) % NZ
+        return pl.ds(((y + dy) % NY) * 16 + (zz % 4) * 4 + zz // 4, 1)
+
+    class Gather:
+        def __init__(self, g):
+            self.g = g
+            self.order = []
+            self.y_in = []
+            self.far_in = []
+            self.z_in = {d: self.send(0, 0, dev_z(d)) for d in (8, 4, 12, 2, 14, 1, 15)}
+            self.to_y(0)
+
+        def send(self, dy, dz, dev):
+            ref = self.g.at[piece(dy, dz)]
+            return rcopy(ref, ref, dev)
+
+        def to_y(self, dz):
+            self.order.append(dz)
+            self.y_in.append({d: self.send(0, dz, dev_y(d)) for d in (1, 3)})
+
+        def arrived(self, copy, dz):
+            copy.wait_recv()
+            self.to_y(dz)
+
+        def near(self):
+            for d, dz in ((1, 15), (15, 1), (2, 14), (14, 2)):
+                self.arrived(self.z_in[d], dz)
+
+        def distant(self):
+            self.z_in[4].wait_recv()
+            low = [self.send(0, 12, dev_z(d)) for d in (1, 15, 2)]
+            self.to_y(12)
+            self.z_in[12].wait_recv()
+            high = [self.send(0, 4, dev_z(d)) for d in (1, 15, 14)]
+            self.to_y(4)
+            self.forward(5)
+            for copy, dz in ((low[0], 11), (high[0], 3), (low[1], 13), (high[1], 5)):
+                self.arrived(copy, dz)
+            self.z_in[8].wait_recv()
+            across = [self.send(0, 8, dev_z(d)) for d in (1, 15)]
+            self.to_y(8)
+            self.arrived(low[2], 10)
+            self.arrived(high[2], 6)
+            self.forward(7)
+            self.arrived(across[0], 7)
+            self.arrived(across[1], 9)
+
+        def forward(self, upto=16):
+            for j in range(len(self.far_in), upto):
+                d = 1 if j % 2 == 0 else 3
+                self.y_in[j][d].wait_recv()
+                self.far_in.append(self.send(4 - d, self.order[j], dev_y(d)))
+
+        def wait(self, d):
+            if d == 2:
+                for copy in self.far_in:
+                    copy.wait_recv()
+            elif d > 0:
+                for j in range(16):
+                    if (j % 2 == 0) != (d == 1):
+                        self.y_in[j][d].wait_recv()
+
+        def block(self, d):
+            yb = (y + 4 - d) % 4
+            rows = self.g[pl.ds(yb * 16, 16)]
+            return yb, rows.astype(F32).reshape(128, 1024).astype(BF16)
 
     def down_block(yb, put):
         for n in range(NC):
@@ -342,16 +364,15 @@
     def use_hidden(n, total):
         hid[:, n * CW : (n + 1) * CW] = res[:, n * CW : (n + 1) * CW].astype(F32) + total
 
-    rs_rest(y_in, rp1, rm1, s1a, ra1, s1b, rb1, use_hidden)
+    rs_rest(y_in, rp1, rm1, s1a, ra1, t1a, t1a, rb1, use_hidden)
 
     mine = y * 16 + k0 * 4 + m0
-    for n in range(NC):
-        cols = slice(n * CW, (n + 1) * CW)
-        nrm[n * 64 + mine] = (hid[:, cols] * gain_ref[:, cols]).astype(BF16)
-    nrm_in = gather_start(nrm)
+    nrm[mine] = (hid[...] * gain_ref[...]).astype(BF16)
+    nrm_all = Gather(nrm)
     h = hid[...]
     ssq[t] = jnp.broadcast_to(jnp.sum(h * h, axis=1, keepdims=True), (8, 128))
     ss_in = [rcopy(ssq.at[t], ssq.at[t], dev_t(d)) for d in (4, 3, 5, 2, 6, 1, 7)]
+    nrm_all.near()
     for copy in ss_in:
         copy.wait_recv()
     square = ssq[0]
@@ -364,7 +385,7 @@
     iv[z] = jnp.sum(jnp.where(spot, inv_rms, 0.0), axis=0, keepdims=True)
     inv_rms = inv_rms[:, :1]
     iv_in = [rcopy(iv.at[z], iv.at[z], dev_z(d)) for d in (8, 7, 9, 6, 10, 5, 11, 4, 12, 3, 13, 2, 14, 1, 15)]
-    y_in = gather_rest(nrm, nrm_in)
+    nrm_all.distant()
     for copy in iv_in:
         copy.wait_recv()
     inv_row = iv[0]
@@ -389,11 +410,10 @@
         def _():
             x_copy(dx).start()
 
-    far_in = None
     blocks = []
     for d in order:
-        gather_wait(y_in, far_in, d)
-        yb, block = gathered(nrm, d)
+        nrm_all.wait(d)
+        yb, block = nrm_all.block(d)
         lhs[...] = block
 
         def columns(j, carry):
@@ -420,7 +440,7 @@
         compact(c, lx.at[yb])
         blocks.append(yb)
         if d == 0:
-            far_in = gather_forward(nrm, y_in)
+            nrm_all.forward()
         if d != 1:
             while blocks:
                 combine(p_in[-len(blocks)], blocks[0])
@@ -580,16 +600,17 @@
         value = inv_rms * (gain_ref[:, cols] * total) - hid[:, cols] * (
             inv_rms * inv_rms * gcol / D
         )
-        dhg[n * 64 + mine] = value.astype(BF16)
-
-    rs_rest(y_in, rp2, rm2, s2a, ra2, s2b, rb2, use_dnormed)
-    y_in = gather_rest(dhg, gather_start(dhg))
+        dhg[mine, :, cols] = value.astype(BF16)
+
+    rs_rest(y_in, rp2, rm2, s2a, ra2, t1b, s2b, rb2, use_dnormed)
+    dhg_all = Gather(dhg)
+    dhg_all.near()
+    dhg_all.distant()
 
     ag_in = {}
-    far_in = None
     for d in order:
-        gather_wait(y_in, far_in, d)
-        yb, block = gathered(dhg, d)
+        dhg_all.wait(d)
+        yb, block = dhg_all.block(d)
         dh[pl.ds(pl.multiple_of(yb * 128, 128), 128), :] = block
         part_a = lax.dot_general(block, w[...], NT, preferred_element_type=F32)
         ags[2 * yb] = part_a[:64]
@@ -597,7 +618,7 @@
         agr[2 * yb] = part_a[:64].astype(BF16)
         agr[2 * yb + 1] = part_a[64:].astype(BF16)
         if d == order[0]:
-            far_in = gather_forward(dhg, y_in)
+            dhg_all.forward()
     for d in (4, 3, 5, 2, 6, 1, 7):
         ag_in[d] = rcopy(agr.at[(t + d) % 8], agr.at[8 + d], dev_t(d))
     for copy in loss_in:
@@ -662,13 +683,13 @@
             v((NC * 16, 8, CW), BF16),
             v((3 * NC * 4, 8, CW), BF16),
             v((NC * 4, 8, CW), F32),
-            v((NC * 4, 8, CW), BF16),
-            v((3 * NC, 8, CW), BF16),
+            v((NC * 4, 8, CW), F32),
+            v((3 * NC, 8, CW), F32),
             v((8, 1024), F32),
             v((8, 8, 128), F32),
             v((NZ, 1, 128), F32),
             v((NY, 1, 128), F32),
-            v((NC * 64, 8, CW), BF16),
+            v((64, 8, 1024), BF16),
             v((NC * 64, 8, CW), BF16),
             v((NC * 16, 8, CW), BF16),
             v((NC * 16, 8, CW), BF16),
@@ -677,7 +698,7 @@
             v((3 * NC * 4, 8, CW), BF16),
             v((NC * 4, 8, CW), BF16),
             v((3 * NC, 8, CW), BF16),
-            v((NC * 64, 8, CW), BF16),
+            v((64, 8, 1024), BF16),
             v((128, 1024), BF16),
             v((128, 1280), F32),
             v((4, 64, CAP * BLK), F32),

time: 150 us -> 148 us (0.987)
  no operation moved by 1% of the time
where the time goes in v3:
time: 148 us
  Pallas kernels  148 us (100%)
    pallas_call x1, Pallas kernels, body(): pl.pallas_call(kernel, out_shape=(jax.ShapeDtypeStruct((256, 512), BF16),...  145 us

profile of v3, /device:TPU:1, one launch (start us, length us, event | category | flops | bytes accessed | tf_op | source)
XLA Modules:
  0.0 148.2 jit_solution(12909842523941828583)
XLA Ops:
  0.6 145.1 %step.1 = (bf16[256,512]{1,0:T(8,128)(2,1)}, bf16[512,1024]{1,0:T(8,128)(2,1)}, bf16[64,256]{1,0:T(8,128)(2,1)}, f32[8,128]{1,0:T(8,128)}) custom-call(bf16[64,8,1024]{2,1,0:T(8,128)(2,1)} %bitcast.5, bf16[64,256]{1,0:T(8,128)(2,1)} %act_hbm.1, bf16[256,1024]{1,0:T(8,128)(2,1)} %w_hbm.1, f32[1,1024]{1,0:T(1,128)} %bitcast.7, bf16[1024,1280]{1,0:T(8,128)(2,1)} %head_hbm.1, ...), custom_call_target="tpu_custom_call" | custom-call | tf_op jit(solution)/shard_map/step/pallas_call | solution.py:660
  145.7 2.5 %last.1 = (f32[1,1]{1,0:T(1,128)}, bf16[256,1024]{1,0:T(8,128)(2,1)}, bf16[64,256]{1,0:T(8,128)(2,1)}) custom-call(bf16[256,512]{1,0:T(8,128)(2,1)} %get-tuple-element.10.actt, bf16[512,1024]{1,0:T(8,128)(2,1)} %get-tuple-element.11.dh, bf16[64,256]{1,0:T(8,128)(2,1)} %get-tuple-element.12.ag, f32[8,128]{1,0:T(8,128)} %get-tuple-element.13.loss), custom_call_target="tpu_custom_call" | custom-call | tf_op jit(solution)/shard_map/last/pallas_call | solution.py:736

commit v4 on v3

--- a/solution.py
+++ b/solution.py
@@ -32,10 +32,11 @@
     tok_ref,
     len_ref,
     adv_ref,
+    dg_ref,
+    ag_ref,
+    loss_ref,
     actt,
     dh,
-    ag_ref,
-    loss_ref,
     res,
     act,
     w,
@@ -183,10 +184,15 @@
     loads[0].wait()
     pl.semaphore_wait(barrier, len(peers))
 
-    a_in = [rcopy(act.at[t], act.at[t], dev_t(d)) for d in (4, 3, 5, 2, 6, 1, 7)]
+    act_at = reserve(8)
+
+    def act_copy(d):
+        return described(act.at[t], act.at[t], dev_t(d), act_at + d)
+
+    for d in (4, 3, 5, 2, 6, 1, 7):
+        sends.append(act_copy(d))
+        sends[-1].start()
     loads[1].wait()
-    for copy in a_in:
-        copy.wait_recv()
 
     def act_rows(yb):
         return jnp.concatenate([act[2 * yb], act[2 * yb + 1]], axis=0)
@@ -352,6 +358,13 @@
             return yb, rows.astype(F32).reshape(128, 1024).astype(BF16)
 
     def down_block(yb, put):
+        for half in range(2):
+            d = (t + 8 - (2 * yb + half)) % 8
+
+            @pl.when(d != 0)
+            def _(d=d):
+                act_copy(d).wait_recv()
+
         for n in range(NC):
             part = jnp.dot(act_rows(yb), w[:, n * CW : (n + 1) * CW], preferred_element_type=F32)
             put(n, slice(None), part.reshape(16, 8, CW))
@@ -607,7 +620,11 @@
     dhg_all.near()
     dhg_all.distant()
 
-    ag_in = {}
+    ag_at = reserve(8)
+
+    def ag_copy(d):
+        return described(agr.at[(t + d) % 8], agr.at[8 + d], dev_t(d), ag_at + d)
+
     for d in order:
         dhg_all.wait(d)
         yb, block = dhg_all.block(d)
@@ -617,10 +634,16 @@
         ags[2 * yb + 1] = part_a[64:]
         agr[2 * yb] = part_a[:64].astype(BF16)
         agr[2 * yb + 1] = part_a[64:].astype(BF16)
+        for half in range(2):
+            to = (2 * yb + half + 8 - t) % 8
+
+            @pl.when(to != 0)
+            def _(to=to):
+                ag_copy(to).start()
+
         if d == order[0]:
             dhg_all.forward()
-    for d in (4, 3, 5, 2, 6, 1, 7):
-        ag_in[d] = rcopy(agr.at[(t + d) % 8], agr.at[8 + d], dev_t(d))
+    dg_ref[...] = jnp.dot(actt[...], dh[...], preferred_element_type=F32).astype(BF16)
     for copy in loss_in:
         copy.wait_recv()
     objective = los[0]
@@ -629,15 +652,17 @@
     loss_ref[...] = -objective / length_sum.astype(F32)
     total = ags[t]
     for d in range(1, 8):
-        ag_in[d].wait_recv()
+        ag_copy(d).wait_recv()
         total = total + agr[8 + d].astype(F32)
     ag_ref[...] = total.astype(BF16)
+    for d in range(1, 8):
+        ag_copy(d).wait_send()
     for copy in sends:
         copy.wait_send()
 
 
-def last(actt, dh, ag, loss, loss_ref, dg_ref, ag_ref):
-    dg_ref[...] = jnp.dot(actt[...], dh[...], preferred_element_type=F32).astype(BF16)
+def last(dg, ag, loss, loss_ref, dg_ref, ag_ref):
+    dg_ref[...] = dg[...]
     ag_ref[...] = ag[...]
     loss_ref[...] = loss[0:1, 0:1]
 
@@ -660,14 +685,15 @@
     out = pl.pallas_call(
         kernel,
         out_shape=(
-            jax.ShapeDtypeStruct((256, 512), BF16),
-            jax.ShapeDtypeStruct((512, 1024), BF16),
+            jax.ShapeDtypeStruct((256, 1024), BF16),
             jax.ShapeDtypeStruct((64, 256), BF16),
             jax.ShapeDtypeStruct((8, 128), F32),
         ),
         in_specs=[any_spec, any_spec, any_spec, vmem, any_spec, vmem, vmem, smem, smem],
-        out_specs=(vmem, vmem, vmem, vmem),
+        out_specs=(vmem, vmem, vmem),
         scratch_shapes=[
+            v((256, 512), BF16),
+            v((512, 1024), BF16),
             v((8, 1024), BF16),
             v((8, 64, 256), BF16),
             v((256, 1024), BF16),
@@ -740,7 +766,7 @@
             jax.ShapeDtypeStruct((256, 1024), BF16),
             jax.ShapeDtypeStruct((64, 256), BF16),
         ),
-        in_specs=[vmem] * 4,
+        in_specs=[vmem] * 3,
         out_specs=(vmem, vmem, vmem),
         name="last",
     )(*out)

time: 148 us -> 145 us (0.980)
  the two profiles are of different devices: /device:TPU:1 before, /device:TPU:17 now
where the time goes in v4:
time: 145 us
  Pallas kernels  144 us (99%)
    pallas_call x1, Pallas kernels, body(): pl.pallas_call(kernel, out_shape=(jax.ShapeDtypeStruct((256, 1024), BF16)...  142 us

profile of v4, /device:TPU:17, one launch (start us, length us, event | category | flops | bytes accessed | tf_op | source)
XLA Modules:
  0.0 144.6 jit_solution(10840082707041063770)
XLA Ops:
  0.6 142.1 %step.1 = (bf16[256,1024]{1,0:T(8,128)(2,1)}, bf16[64,256]{1,0:T(8,128)(2,1)}, f32[8,128]{1,0:T(8,128)}) custom-call(bf16[64,8,1024]{2,1,0:T(8,128)(2,1)} %bitcast.5, bf16[64,256]{1,0:T(8,128)(2,1)} %act_hbm.1, bf16[256,1024]{1,0:T(8,128)(2,1)} %w_hbm.1, f32[1,1024]{1,0:T(1,128)} %bitcast.7, bf16[1024,1280]{1,0:T(8,128)(2,1)} %head_hbm.1, ...), custom_call_target="tpu_custom_call" | custom-call | tf_op jit(solution)/shard_map/step/pallas_call | solution.py:685
  142.7 1.9 %last.1 = (f32[1,1]{1,0:T(1,128)}, bf16[256,1024]{1,0:T(8,128)(2,1)}, bf16[64,256]{1,0:T(8,128)(2,1)}) custom-call(bf16[256,1024]{1,0:T(8,128)(2,1)} %get-tuple-element.9.dg, bf16[64,256]{1,0:T(8,128)(2,1)} %get-tuple-element.10.ag, f32[8,128]{1,0:T(8,128)} %get-tuple-element.11.loss), custom_call_target="tpu_custom_call" | custom-call | tf_op jit(solution)/shard_map/last/pallas_call | solution.py:762

commit v5 on v4

--- a/solution.py
+++ b/solution.py
@@ -565,7 +565,13 @@
         hot = jnp.where((tok_slot == float(s)) & (lane == tok_lane), 1.0, 0.0)
         dl[t, :, s * BLK : (s + 1) * BLK] = (weight * (prob - hot)).astype(BF16)
     dx_in = {d: rcopy(dl.at[t], dl.at[t], dev_x(d)) for d in (2, 1, 3)}
-    d_in = {0: rcopy(dl.at[t], dl.at[t], partner)}
+    dl_at = reserve(4)
+
+    def to_partner(slot, d):
+        return described(dl.at[slot], dl.at[slot], partner, dl_at + d)
+
+    sends.append(to_partner(t, 0))
+    sends[-1].start()
     gv[t] = to_row(gdot)
     g_in = [rcopy(gv.at[t], gv.at[t], dev_t(d)) for d in (4, 3, 5, 2, 6, 1, 7)]
     los[t] = jnp.broadcast_to(part, (8, 128))
@@ -573,11 +579,11 @@
     for d in (1, 3, 2):
         dx_in[d].wait_recv()
         slot = ((x + 4 - d) % 4) * 2 + c
-        d_in[d] = rcopy(dl.at[slot], dl.at[slot], partner)
-    for d in range(4):
-        d_in[d].wait_recv()
+        sends.append(to_partner(slot, d))
+        sends[-1].start()
 
     def head_block(yb, put):
+        to_partner(t, (x + 4 - yb) % 4).wait_recv()
         for half in range(2):
             rows = slice(half * 64, (half + 1) * 64)
             mask_rows = pl.ds(pl.multiple_of(yb * 128 + half * 64, 64), 64)

time: 145 us -> 144 us (level)
  no operation moved by 1% of the time
where the time goes in v5:
time: 144 us
  Pallas kernels  143 us (99%)
    pallas_call x1, Pallas kernels, body(): pl.pallas_call(kernel, out_shape=(jax.ShapeDtypeStruct((256, 1024), BF16)...  141 us

profile of v5, /device:TPU:17, one launch (start us, length us, event | category | flops | bytes accessed | tf_op | source)
XLA Modules:
  0.0 144.0 jit_solution(11879167081800848933)
XLA Ops:
  0.6 141.5 %step.1 = (bf16[256,1024]{1,0:T(8,128)(2,1)}, bf16[64,256]{1,0:T(8,128)(2,1)}, f32[8,128]{1,0:T(8,128)}) custom-call(bf16[64,8,1024]{2,1,0:T(8,128)(2,1)} %bitcast.5, bf16[64,256]{1,0:T(8,128)(2,1)} %act_hbm.1, bf16[256,1024]{1,0:T(8,128)(2,1)} %w_hbm.1, f32[1,1024]{1,0:T(1,128)} %bitcast.7, bf16[1024,1280]{1,0:T(8,128)(2,1)} %head_hbm.1, ...), custom_call_target="tpu_custom_call" | custom-call | tf_op jit(solution)/shard_map/step/pallas_call | solution.py:691
  142.1 1.9 %last.1 = (f32[1,1]{1,0:T(1,128)}, bf16[256,1024]{1,0:T(8,128)(2,1)}, bf16[64,256]{1,0:T(8,128)(2,1)}) custom-call(bf16[256,1024]{1,0:T(8,128)(2,1)} %get-tuple-element.9.dg, bf16[64,256]{1,0:T(8,128)(2,1)} %get-tuple-element.10.ag, f32[8,128]{1,0:T(8,128)} %get-tuple-element.11.loss), custom_call_target="tpu_custom_call" | custom-call | tf_op jit(solution)/shard_map/last/pallas_call | solution.py:768
